TPU v7x, 32 devices: a whole 2x2x4 slice. The times are simulated.
32 devices in a mesh: node: 8 (over z, x), mp: 4 (over y, core).
Axes of the slice: x: 2, y: 2, z: 4, core: 2. Of those that a mesh axis runs over, the one named last changes fastest.
Arguments:
- queries: bfloat16 [32, 64, 128], P('node', 'mp'), may hold values from -8 to 8
- root_keys: bfloat16 [16384, 8, 128], P('node', 'mp'), may hold values from -6 to 6
- root_values: bfloat16 [16384, 8, 128], P('node', 'mp'), may hold values from -6 to 6
- mid_keys: bfloat16 [8, 1024, 8, 128], P('node', None, 'mp'), may hold values from -6 to 6
- mid_values: bfloat16 [8, 1024, 8, 128], P('node', None, 'mp'), may hold values from -6 to 6
- leaf_keys: bfloat16 [32, 256, 8, 128], P('node', None, 'mp'), may hold values from -6 to 6
- leaf_values: bfloat16 [32, 256, 8, 128], P('node', None, 'mp'), may hold values from -6 to 6
- mid_length: int32 [8], replicated, may hold values from 1 to 1024
- leaf_length: int32 [32], P('node'), may hold values from 1 to 256
- branch_mid: int32 [32, 1], replicated, may hold values from 0 to 7; in each aligned block of 32 rows (0 to 31, 32 to 63, ...) at most 8 rows name the same one
- residual: bfloat16 [32, 8192], P(None, 'node'), may hold values from -6 to 6
- norm_gain: float32 [8192], P('node'), may hold values from 0.5 to 1.5
- out_weight: bfloat16 [8192, 8192], P('mp', 'node'), may hold values from -0.0625 to 0.0625
- gate_weight: bfloat16 [8192, 28672], P('node', 'mp'), may hold values from -0.0625 to 0.0625
- up_weight: bfloat16 [8192, 28672], P('node', 'mp'), may hold values from -0.0625 to 0.0625
- down_weight: bfloat16 [28672, 8192], P('mp', 'node'), may hold values from -0.03125 to 0.03125
Outputs:
- layer_out: bfloat16 [32, 8192], P('mp', 'node')
Inputs may be any that keep to these rules, and one draw needn't show every extreme that they name: `branch_mid`: every inner tree node lies on the path of 1 to 8 branches, and some node on exactly 8.
All inputs are finite; a program needn't handle non-finite values.
Results may differ from a plain program's by a relative error of at most 0.015.
Values may be sent and summed in bfloat16 or wider, within the bound.
A program may use at most 128 MiB of HBM per device.

v0:
```python
import functools
import math

import jax
import jax.numpy as jnp
import numpy as np
from jax import lax
from jax.experimental import pallas as pl
from jax.experimental.pallas import tpu as pltpu
from jax.sharding import PartitionSpec as P

norm_eps = 1e-05
masked_score = -1e30
MESH = pl.DeviceIdType.MESH
ROWS = 128


def nt_dot(a, b):
    return lax.dot_general(a, b, (((1,), (1,)), ((), ())), preferred_element_type=jnp.float32)


def nn_dot(a, b):
    return jnp.dot(a, b, preferred_element_type=jnp.float32)


def layer_kernel(
    n, mp, owners, scale2,
    q_ref, mid_lo, mid_hi, leaf_lo, leaf_hi, spread_ref, order_ref, res_ref, gain_ref,
    rk_hbm, rv_hbm, mk_hbm, mv_hbm, lk_hbm, lv_hbm, ow_hbm, gw_hbm, uw_hbm, dw_hbm,
    out_ref,
    raw, keys, values, ow, gw, uw, dw,
    qall, part_send, part_recv, leaf_part, att_own, att_all, lhs, pr_own, pr_all, stream,
    sq_own, sq_all, xg, gu_send, gu_recv, act_all, acc, dn_send, dn_recv,
    kv_sem, w_sem, q_s, q_r, p_s, p_r, a_s, a_r, s_s, s_r, g_s, g_r, c_s, c_r, o_s, o_r, d_s, d_r,
):
    me = lax.axis_index("node")
    mpi = lax.axis_index("mp")
    heads, own_rows, hd = q_ref.shape
    chunk = act_all.shape[2]
    width = stream.shape[1]
    root = rk_hbm.shape[0] // heads
    mids = mk_hbm.shape[0] // heads
    leaves = lk_hbm.shape[0] // heads
    shared = root + mids

    kv_copies = []
    for side, (a, b, c) in enumerate(((rk_hbm, mk_hbm, lk_hbm), (rv_hbm, mv_hbm, lv_hbm))):
        start = 0
        for k, src in enumerate((a, b, c)):
            size = src.shape[0]
            copy = pltpu.make_async_copy(
                src, raw.at[side, pl.ds(start, size)], kv_sem.at[side * 3 + k]
            )
            copy.start()
            kv_copies.append(copy)
            start += size
    w_copies = []
    for k, (src, dst) in enumerate(((ow_hbm, ow), (gw_hbm, gw), (uw_hbm, uw), (dw_hbm, dw))):
        copy = pltpu.make_async_copy(src, dst, w_sem.at[k])
        copy.start()
        w_copies.append(copy)

    barrier = pltpu.get_barrier_semaphore()

    def greet(axis, here, count):
        def body(i, carry):
            pl.semaphore_signal(
                barrier, inc=1, device_id={axis: lax.rem(here + i, count)}, device_id_type=MESH
            )
            return carry

        lax.fori_loop(1, count, body, 0)

    greet("node", me, n)
    greet("mp", mpi, mp)
    pl.semaphore_wait(barrier, n - 1 + mp - 1)

    def remote(src, dst, send, recv, axis, peer):
        return pltpu.make_async_remote_copy(
            src_ref=src, dst_ref=dst, send_sem=send, recv_sem=recv,
            device_id={axis: peer}, device_id_type=MESH,
        )

    def peers(axis, fn):
        here, count = (me, n) if axis == "node" else (mpi, mp)

        def body(i, carry):
            fn(lax.rem(here + i, count))
            return carry

        lax.fori_loop(1, count, body, 0)

    def send_all(axis, src, dst, send, recv):
        here = me if axis == "node" else mpi
        peers(
            axis,
            lambda j: remote(src(j), dst.at[here], send.at[j], recv.at[here], axis, j).start(),
        )

    def wait_all(axis, src, dst, send, recv):
        peers(axis, lambda j: remote(src(j), dst.at[j], send.at[j], recv.at[j], axis, j).wait())

    send_all("node", lambda j: q_ref, qall, q_s, q_r)
    qall[me] = q_ref[...]

    for copy in kv_copies:
        copy.wait()
    block = spread_ref.shape[0]
    per = block // heads

    def split(i, carry):
        at = pl.ds(pl.multiple_of(i * block, block), block)
        to = pl.ds(pl.multiple_of(i * per, per), per)
        for side, dst in enumerate((keys, values)):
            rows = nn_dot(spread_ref[...], raw[side, at, :]).astype(jnp.bfloat16)
            for h in range(heads):
                dst[h, to, :] = rows[h * per:(h + 1) * per]
        return carry

    lax.fori_loop(0, raw.shape[1] // block, split, 0)

    def leaf_attend(h):
        scores = nt_dot(q_ref[h], keys[h, shared:, :])
        slot = lax.broadcasted_iota(jnp.int32, scores.shape, 1)
        seen = (slot >= leaf_lo[...]) & (slot < leaf_hi[...])
        scores = jnp.where(seen, scores, masked_score)
        peak = jnp.max(scores, axis=1, keepdims=True)
        weights = jnp.where(seen, jnp.exp2((scores - peak) * scale2), 0.0)
        total = jnp.sum(weights, axis=1, keepdims=True)
        weighted = nn_dot(weights.astype(jnp.bfloat16), values[h, shared:, :])
        lane = lax.broadcasted_iota(jnp.int32, (own_rows, hd), 1)
        leaf_part[h, :, 0:hd] = weighted
        leaf_part[h, :, hd:] = jnp.where(lane == 0, peak, total)

    for h in range(heads):
        leaf_attend(h)

    wait_all("node", lambda j: q_ref, qall, q_s, q_r)

    group = max(1, min(n, ROWS // own_rows))
    rows = group * own_rows

    def attend(i, carry):
        picks = pl.ds(i * group, group)
        at = pl.ds(pl.multiple_of(i * rows, rows), rows)
        low, high = mid_lo[at, :], mid_hi[at, :]
        for h in range(heads):
            query = qall[picks, h].reshape(rows, hd)
            root_scores = nt_dot(query, keys[h, 0:root, :])
            mid_scores = nt_dot(query, keys[h, root:shared, :])
            slot = lax.broadcasted_iota(jnp.int32, mid_scores.shape, 1)
            seen = (slot >= low) & (slot < high)
            mid_scores = jnp.where(seen, mid_scores, masked_score)
            peak = jnp.maximum(
                jnp.max(root_scores, axis=1, keepdims=True),
                jnp.max(mid_scores, axis=1, keepdims=True),
            )
            root_weights = jnp.exp2((root_scores - peak) * scale2)
            mid_weights = jnp.where(seen, jnp.exp2((mid_scores - peak) * scale2), 0.0)
            total = jnp.sum(root_weights, axis=1, keepdims=True) + jnp.sum(
                mid_weights, axis=1, keepdims=True
            )
            weighted = nn_dot(root_weights.astype(jnp.bfloat16), values[h, 0:root, :]) + nn_dot(
                mid_weights.astype(jnp.bfloat16), values[h, root:shared, :]
            )
            lane = lax.broadcasted_iota(jnp.int32, (rows, hd), 1)
            side = jnp.where(lane == 0, peak, total)
            part_send[picks, h, :, 0:hd] = weighted.reshape(group, own_rows, hd)
            part_send[picks, h, :, hd:] = side.reshape(group, own_rows, hd)
        return carry

    lax.fori_loop(0, n // group, attend, 0)
    send_all("node", lambda j: part_send.at[j], part_recv, p_s, p_r)
    part_recv[me] = part_send[me]
    wait_all("node", lambda j: part_send.at[j], part_recv, p_s, p_r)

    for h in range(heads):
        def merge(i, carry):
            peak, total, weighted = carry
            peak_i = part_recv[i, h, :, hd:hd + 1]
            total_i = part_recv[i, h, :, hd + 1:hd + 2]
            top = jnp.maximum(peak, peak_i)
            one, two = jnp.exp2((peak - top) * scale2), jnp.exp2((peak_i - top) * scale2)
            return (
                top,
                total * one + total_i * two,
                weighted * one + part_recv[i, h, :, 0:hd] * two,
            )

        first = (
            leaf_part[h, :, hd:hd + 1],
            leaf_part[h, :, hd + 1:hd + 2],
            leaf_part[h, :, 0:hd],
        )
        _, total, weighted = lax.fori_loop(0, n, merge, first)
        att_own[h] = (weighted / total).astype(jnp.bfloat16)

    send_all("node", lambda j: att_own, att_all, a_s, a_r)
    att_all[me] = att_own[...]
    wait_all("node", lambda j: att_own, att_all, a_s, a_r)

    branches = lhs.shape[0]
    size = n * own_rows // branches
    for h in range(heads):
        mixed = att_all[:, h].reshape(n * own_rows, hd)
        mixed = nn_dot(order_ref[...], mixed).astype(jnp.bfloat16)
        for g in range(size):
            first = (h * size + g) * hd
            lhs[:, first:first + hd] = mixed[g * branches:(g + 1) * branches]

    w_copies[0].wait()
    tile = math.gcd(width, 256)

    def project(i, carry):
        at = pl.ds(pl.multiple_of(i * tile, tile), tile)
        pr_own[:, at] = nn_dot(lhs[...], ow[:, at]).astype(jnp.bfloat16)
        return carry

    lax.fori_loop(0, width // tile, project, 0)
    send_all("mp", lambda j: pr_own, pr_all, o_s, o_r)
    pr_all[mpi] = pr_own[...]
    wait_all("mp", lambda j: pr_own, pr_all, o_s, o_r)
    total = pr_all[0].astype(jnp.float32)
    for k in range(1, mp):
        total = total + pr_all[k].astype(jnp.float32)
    total = res_ref[...].astype(jnp.float32) + total
    stream[...] = total
    squares = jnp.sum(total * total, axis=1, keepdims=True)
    sq_own[...] = jnp.broadcast_to(squares, sq_own.shape)
    send_all("node", lambda j: sq_own, sq_all, s_s, s_r)
    sq_all[me] = sq_own[...]
    xg[...] = (total * gain_ref[...]).astype(jnp.bfloat16)

    w_copies[1].wait()
    w_copies[2].wait()

    def gate_up(i, carry):
        j = lax.rem(me + 1 + i, owners)
        at = pl.ds(pl.multiple_of(j * chunk, 128), chunk)
        gate = nn_dot(xg[...], gw[:, at]).astype(jnp.bfloat16)
        upward = nn_dot(xg[...], uw[:, at]).astype(jnp.bfloat16)
        gu_send[j, 0] = gate
        gu_send[j, 1] = upward

        @pl.when(j != me)
        def _():
            remote(gu_send.at[j], gu_recv.at[me], g_s.at[j], g_r.at[me], "node", j).start()

        return carry

    lax.fori_loop(0, owners, gate_up, 0)
    wait_all("node", lambda j: sq_own, sq_all, s_s, s_r)

    def owner_work():
        gu_recv[me] = gu_send[me]
        peers(
            "node",
            lambda j: remote(gu_send.at[0], gu_recv.at[j], g_s.at[0], g_r.at[j], "node", j).wait_recv(),
        )
        squares = sq_all[0][:, 0:1]
        for k in range(1, n):
            squares = squares + sq_all[k][:, 0:1]
        root_mean = lax.rsqrt(squares / (width * n) + norm_eps)

        def add(i, carry):
            return (
                carry[0] + gu_recv[i, 0].astype(jnp.float32),
                carry[1] + gu_recv[i, 1].astype(jnp.float32),
            )

        zero = jnp.zeros((branches, chunk), jnp.float32)
        gate, upward = lax.fori_loop(0, n, add, (zero, zero))
        gate, upward = gate * root_mean, upward * root_mean
        act_all[me] = (gate / (1.0 + jnp.exp(-gate)) * upward).astype(jnp.bfloat16)
        send_all("node", lambda j: act_all.at[me], act_all, c_s, c_r)

    if owners == n:
        owner_work()
    else:
        pl.when(me < owners)(owner_work)

    w_copies[3].wait()
    acc[...] = jnp.zeros(acc.shape, jnp.float32)

    def down(i, carry):
        j = lax.rem(me + i, n)

        def step():
            @pl.when(j != me)
            def _():
                remote(act_all.at[j], act_all.at[j], c_s.at[j], c_r.at[j], "node", j).wait_recv()

            at = pl.ds(pl.multiple_of(j * chunk, 128), chunk)
            acc[...] += nn_dot(act_all[j], dw[at, :])

        if owners == n:
            step()
        else:
            pl.when(j < owners)(step)
        return carry

    lax.fori_loop(0, n, down, 0)

    rows_out = out_ref.shape[0]
    for k in range(mp):
        dn_send[k] = acc[k * rows_out:(k + 1) * rows_out, :].astype(jnp.bfloat16)
    send_all("mp", lambda j: dn_send.at[j], dn_recv, d_s, d_r)
    dn_recv[mpi] = dn_send[mpi]
    wait_all("mp", lambda j: dn_send.at[j], dn_recv, d_s, d_r)
    total = dn_recv[0].astype(jnp.float32)
    for k in range(1, mp):
        total = total + dn_recv[k].astype(jnp.float32)
    own = stream[pl.ds(pl.multiple_of(mpi * rows_out, rows_out), rows_out), :]
    out_ref[...] = (own + total).astype(jnp.bfloat16)

    def sent(i, carry):
        j = lax.rem(me + 1 + i, owners)

        @pl.when(j != me)
        def _():
            remote(gu_send.at[j], gu_recv.at[me], g_s.at[j], g_r.at[me], "node", j).wait_send()

        return carry

    lax.fori_loop(0, owners, sent, 0)

    def acts_sent():
        peers(
            "node",
            lambda j: remote(act_all.at[me], act_all.at[me], c_s.at[j], c_r.at[j], "node", j).wait_send(),
        )

    if owners == n:
        acts_sent()
    else:
        pl.when(me < owners)(acts_sent)


def on_device(
    n, mp,
    queries, root_keys, root_values, mid_keys, mid_values, leaf_keys, leaf_values,
    mid_length, leaf_length, branch_mid, residual, norm_gain,
    out_weight, gate_weight, up_weight, down_weight,
):
    owned, local_heads, hd = queries.shape
    heads = root_keys.shape[1]
    size = local_heads // heads
    own_rows = owned * size
    branches = owned * n
    width = residual.shape[1]
    hidden = gate_weight.shape[1]
    lane_tiles = hidden // 128
    owners = max(k for k in range(1, n + 1) if lane_tiles % k == 0)
    chunk = hidden // owners
    mid_slots = mid_keys.shape[1]
    leaf_slots = leaf_keys.shape[1]
    local_mids = mid_keys.shape[0]

    q = queries.reshape(owned, heads, size, hd).transpose(1, 0, 2, 3).reshape(heads, own_rows, hd)
    local = branch_mid[:, 0] - lax.axis_index("node") * local_mids
    here = (local >= 0) & (local < local_mids)
    mid_lo = jnp.where(here, local * mid_slots, 0)
    mid_hi = jnp.where(here, mid_lo + mid_length[branch_mid[:, 0]], 0)
    mid_lo = jnp.repeat(mid_lo, size)[:, None]
    mid_hi = jnp.repeat(mid_hi, size)[:, None]
    leaf_lo = jnp.arange(owned, dtype=jnp.int32) * leaf_slots
    leaf_hi = jnp.repeat(leaf_lo + leaf_length, size)[:, None]
    leaf_lo = jnp.repeat(leaf_lo, size)[:, None]

    block = 128 * heads
    spread = np.zeros((block, block), np.float32)
    at = np.arange(block)
    spread[(at % heads) * 128 + at // heads, at] = 1.0
    order = np.zeros((branches * size, branches * size), np.float32)
    at = np.arange(branches * size)
    order[(at % size) * branches + at // size, at] = 1.0

    flat = [
        a.reshape(-1, hd)
        for a in (root_keys, root_values, mid_keys, mid_values, leaf_keys, leaf_values)
    ]
    raw_rows = flat[0].shape[0] + flat[2].shape[0] + flat[4].shape[0]
    bf, f32 = jnp.bfloat16, jnp.float32
    dma = pltpu.SemaphoreType.DMA
    vmem = pl.BlockSpec(memory_space=pltpu.VMEM)
    hbm = pl.BlockSpec(memory_space=pl.ANY)
    rows_out = branches // mp
    scratch = [
        pltpu.VMEM((2, raw_rows, hd), bf),
        pltpu.VMEM((heads, raw_rows // heads, hd), bf),
        pltpu.VMEM((heads, raw_rows // heads, hd), bf),
        pltpu.VMEM(out_weight.shape, bf),
        pltpu.VMEM(gate_weight.shape, bf),
        pltpu.VMEM(up_weight.shape, bf),
        pltpu.VMEM(down_weight.shape, bf),
        pltpu.VMEM((n, heads, own_rows, hd), bf),
        pltpu.VMEM((n, heads, own_rows, 2 * hd), f32),
        pltpu.VMEM((n, heads, own_rows, 2 * hd), f32),
        pltpu.VMEM((heads, own_rows, 2 * hd), f32),
        pltpu.VMEM((heads, own_rows, hd), bf),
        pltpu.VMEM((n, heads, own_rows, hd), bf),
        pltpu.VMEM((branches, local_heads * hd), bf),
        pltpu.VMEM((branches, width), bf),
        pltpu.VMEM((mp, branches, width), bf),
        pltpu.VMEM((branches, width), f32),
        pltpu.VMEM((branches, 128), f32),
        pltpu.VMEM((n, branches, 128), f32),
        pltpu.VMEM((branches, width), bf),
        pltpu.VMEM((owners, 2, branches, chunk), bf),
        pltpu.VMEM((n, 2, branches, chunk), bf),
        pltpu.VMEM((owners, branches, chunk), bf),
        pltpu.VMEM((branches, width), f32),
        pltpu.VMEM((mp, rows_out, width), bf),
        pltpu.VMEM((mp, rows_out, width), bf),
        dma((6,)),
        dma((4,)),
    ] + [dma((n,))] * 12 + [dma((mp,))] * 4
    scale2 = hd ** -0.5 * math.log2(math.e)
    return pl.pallas_call(
        functools.partial(layer_kernel, n, mp, owners, scale2),
        out_shape=jax.ShapeDtypeStruct((rows_out, width), bf),
        in_specs=[vmem] * 9 + [hbm] * 10,
        out_specs=vmem,
        scratch_shapes=scratch,
        compiler_params=pltpu.CompilerParams(
            collective_id=0, has_side_effects=True, vmem_limit_bytes=67043328
        ),
    )(
        q, mid_lo, mid_hi, leaf_lo, leaf_hi,
        jnp.asarray(spread, bf), jnp.asarray(order, bf), residual, norm_gain[None, :],
        *flat, out_weight, gate_weight, up_weight, down_weight,
    )


def solution(mesh):
    in_specs = (
        P("node", "mp", None),
        P("node", "mp", None),
        P("node", "mp", None),
        P("node", None, "mp", None),
        P("node", None, "mp", None),
        P("node", None, "mp", None),
        P("node", None, "mp", None),
        P(),
        P("node"),
        P(),
        P(None, "node"),
        P("node"),
        P("mp", "node"),
        P("node", "mp"),
        P("node", "mp"),
        P("mp", "node"),
    )
    body = functools.partial(on_device, mesh.shape["node"], mesh.shape["mp"])
    return jax.shard_map(
        body, mesh=mesh, in_specs=in_specs, out_specs=P("mp", "node"), check_vma=False
    )
```

profile of v0, /device:TPU:19, one launch (start us, length us, event | category | flops | bytes accessed | tf_op | source)
XLA Modules:
  0.0 105.1 jit_solution(5305765897236295571)
XLA Ops:
  0.0 0.7 fusion.1
  0.7 0.7 fusion
  1.3 0.1 broadcast_in_dim.21
  1.4 0.1 broadcast_in_dim.22
  1.5 1.4 %gather_fusion = s32[32]{0:T(128)S(1)} fusion(s32[8]{0:T(128)} %param.25, s32[1024]{0:T(1024)S(1)} %pad_clamp_fusion), kind=kCustom, calls=%fused_computation | custom fusion | bytes 384 | tf_op jit(solution)/shard_map/gather | solution.py:363
  2.8 0.7 bitcast_select_fusion
  3.5 0.7 broadcast_in_dim_reshape.19.leaf_hi
  4.2 0.7 broadcast_in_dim_reshape.18.leaf_lo
  4.8 0.1 broadcast_in_dim.20
  4.9 0.1 broadcast_in_dim.19
  5.0 1.3 %copy_bitcast_fusion.q_ref = bf16[2,32,128]{2,1,0:T(8,128)(2,1)} fusion(bf16[4,16,128]{2,1,0:T(8,128)(2,1)} %param.18), kind=kLoop, calls=%fused_computation.1 | loop fusion | bytes 32768 | tf_op jit(solution)/shard_map/reshape | solution.py:359
  6.3 0.7 broadcast_in_dim_reshape.16.mid_lo
  7.1 0.7 broadcast_in_dim_reshape.17.mid_hi
  7.8 95.9 %shard_map.172 = bf16[8,1024]{1,0:T(8,128)(2,1)} custom-call(bf16[2,32,128]{2,1,0:T(8,128)(2,1)} %copy_bitcast_fusion.q_ref, s32[256,1]{1,0:T(8,128)} %broadcast_in_dim_reshape.16.mid_lo, s32[256,1]{1,0:T(8,128)} %broadcast_in_dim_reshape.17.mid_hi, s32[32,1]{1,0:T(8,128)} %broadcast_in_dim_reshape.18.leaf_lo, s32[32,1]{1,0:T(8,128)} %broadcast_in_dim_reshape.19.leaf_hi, ...), custom_call_target="tpu_custom_call" | custom-call | tf_op jit(solution)/shard_map/pallas_call | solution.py:419
  103.7 1.3 %copy.29 = bf16[8,1024]{1,0:T(8,128)(2,1)} copy(bf16[8,1024]{1,0:T(8,128)(2,1)} %shard_map.172) | data formatting | bytes 32768
  (2 shorter events, 0.0 us)
where the time goes:
time: 105 us
  Pallas kernels  95.9 us (91%)
  local copies, waits for them, and re-layouts  7.13 us (7%)
  other arithmetic  1.99 us (2%)
    pallas_call x1, Pallas kernels, on_device(): pl.pallas_call(functools.partial(layer_kernel, n, mp, owners, scale2), ou...  95.9 us

commit v1 on v0

v1 whole, which is shorter than its diff:
```python
import functools
import math
from contextlib import nullcontext as scope

import jax
import jax.numpy as jnp
import numpy as np
from jax import lax
from jax.experimental import pallas as pl
from jax.experimental.pallas import tpu as pltpu
from jax.sharding import PartitionSpec as P

norm_eps = 1e-05
masked_score = -1e30
MESH = pl.DeviceIdType.MESH
ROWS = 128


def nt_dot(a, b):
    return lax.dot_general(a, b, (((1,), (1,)), ((), ())), preferred_element_type=jnp.float32)


def nn_dot(a, b):
    return jnp.dot(a, b, preferred_element_type=jnp.float32)


def to_lanes(columns):
    rows = columns[0].shape[0]
    lane = lax.broadcasted_iota(jnp.int32, (rows, 128), 1)
    grid = jnp.zeros((rows, 128), jnp.float32)
    for k, column in enumerate(columns):
        grid = jnp.where(lane == k, column, grid)
    if rows < 128:
        grid = jnp.concatenate([grid] * (128 // rows), axis=0)
    return grid.T


def layer_kernel(
    n, mp, owners, scale2, local_mids, mid_slots, leaf_slots, size, subs,
    mid_of, mid_len, leaf_len,
    q_hbm, order_hbm, res_hbm, gain_hbm,
    rk_hbm, rv_hbm, mk_hbm, mv_hbm, lk_hbm, lv_hbm, ow_hbm, gw_hbm, uw_hbm, dw_hbm,
    out_ref,
    q_raw, order_ref, res_ref, gain_ref, keys, values, ow, gw, uw, dw,
    q_own, qall, part_send, part_recv, st_send, st_recv, leaf_part, fac, att_own, att_all, lhs,
    pr_own, pr_hi, pr_pair, pr_lo, stream, sq_own, sq_all, xg,
    gx_send, gx_recv, own_sum, gz_send, gz_recv, act_all, acc, dn_send, dn_recv,
    in_sem, kv_sem, w_sem, q_s, q_r, p_s, p_r, t_s, t_r, a_s, a_r, s_s, s_r,
    h_s, h_r, l_s, l_r, gx_s, gx_r, gz_s, gz_r, cz_s, cz_r, cx_s, cx_r, d_s, d_r,
):
    me = lax.axis_index("node")
    mpi = lax.axis_index("mp")
    owned, local_heads, hd = q_raw.shape
    heads = local_heads // size
    own_rows = owned * size
    span = heads * hd
    chunk = act_all.shape[2]
    branches, width = stream.shape
    root = rk_hbm.shape[0]
    mids = mk_hbm.shape[0]
    shared = root + mids
    lo, hi = lax.rem(me, 2), me // 2
    partner = me + 1 - 2 * lo
    halves = n // 2
    owner_halves = owners // 2
    mp_lo, mp_hi = lax.rem(mpi, 2), mpi // 2
    mp_partner = mpi + 1 - 2 * mp_lo
    mp_halves = mp // 2

    in_copies = [
        pltpu.make_async_copy(src, dst, in_sem.at[k])
        for k, (src, dst) in enumerate(
            ((q_hbm, q_raw), (order_hbm, order_ref), (res_hbm, res_ref), (gain_hbm, gain_ref))
        )
    ]
    in_copies[0].start()
    kv_copies = []
    for side, (dst, parts) in enumerate(
        ((keys, (rk_hbm, mk_hbm, lk_hbm)), (values, (rv_hbm, mv_hbm, lv_hbm)))
    ):
        start = 0
        for k, src in enumerate(parts):
            rows = src.shape[0]
            copy = pltpu.make_async_copy(
                src, dst.at[pl.ds(start, rows), pl.ds(0, hd)], kv_sem.at[side * 3 + k]
            )
            copy.start()
            kv_copies.append(copy)
            start += rows
    for copy in in_copies[1:]:
        copy.start()
    w_copies = [
        pltpu.make_async_copy(src, dst, w_sem.at[k])
        for k, (src, dst) in enumerate(((ow_hbm, ow), (gw_hbm, gw), (uw_hbm, uw), (dw_hbm, dw)))
    ]

    barrier = pltpu.get_barrier_semaphore()

    def greet(axis, here, count):
        def body(i, carry):
            pl.semaphore_signal(
                barrier, inc=1, device_id={axis: lax.rem(here + i, count)}, device_id_type=MESH
            )
            return carry

        lax.fori_loop(1, count, body, 0)

    greet("node", me, n)
    greet("mp", mpi, mp)

    def remote(src, dst, send, recv, axis, peer):
        return pltpu.make_async_remote_copy(
            src_ref=src, dst_ref=dst, send_sem=send, recv_sem=recv,
            device_id={axis: peer}, device_id_type=MESH,
        )

    def peers(axis, fn):
        here, count = (me, n) if axis == "node" else (mpi, mp)

        def body(i, carry):
            fn(lax.rem(here + i, count))
            return carry

        lax.fori_loop(1, count, body, 0)

    def send_all(axis, src, dst, send, recv):
        here = me if axis == "node" else mpi
        peers(
            axis,
            lambda j: remote(src(j), dst.at[here], send.at[j], recv.at[here], axis, j).start(),
        )

    def wait_sends(axis, src, dst, send, recv):
        peers(axis, lambda j: remote(src(j), dst.at[j], send.at[j], recv.at[j], axis, j).wait_send())

    def wait_recvs(axis, src, dst, send, recv):
        peers(axis, lambda j: remote(src(j), dst.at[j], send.at[j], recv.at[j], axis, j).wait_recv())

    with scope("qprep"):
        in_copies[0].wait()
        raw_q = q_raw[...].astype(jnp.float32)
        for h in range(heads):
            q_own[:, h * hd:(h + 1) * hd] = (
                raw_q[:, h * size:(h + 1) * size, :].reshape(own_rows, hd).astype(jnp.bfloat16)
            )
        qall[me] = q_own[...]

    with scope("barrier"):
        pl.semaphore_wait(barrier, n - 1 + mp - 1)
    send_all("node", lambda j: q_own, qall, q_s, q_r)

    with scope("kvwait"):
        for copy in kv_copies:
            copy.wait()
    for copy in w_copies:
        copy.start()

    block = 256
    row = lax.broadcasted_iota(jnp.int32, (block, hd), 0)
    keep = [(lax.rem(row, heads) == h).astype(jnp.float32).astype(jnp.bfloat16) for h in range(heads)]

    def spread(i, carry):
        at = pl.ds(pl.multiple_of(i * block, block), block)
        for ref in (keys, values):
            mixed = ref[at, 0:hd]
            for h in range(heads):
                ref[at, h * hd:(h + 1) * hd] = mixed * keep[h]
        return carry

    with scope("spread"):
        lax.fori_loop(0, keys.shape[0] // block, spread, 0)

    def softmax_parts(pieces, rows):
        lane = lax.broadcasted_iota(jnp.int32, (rows, 128), 1)
        top = None
        for piece in pieces:
            for k in range(piece.shape[1] // 128):
                part = piece[:, k * 128:(k + 1) * 128]
                top = part if top is None else jnp.maximum(top, part)
        tops, mixed_top = [], None
        for h in range(heads):
            mine = lax.rem(lane, heads) == h
            peak = jnp.max(jnp.where(mine, top, -jnp.inf), axis=1, keepdims=True)
            tops.append(peak)
            mixed_top = jnp.broadcast_to(peak, lane.shape) if h == 0 else jnp.where(mine, peak, mixed_top)
        weights, total = [], None
        for piece in pieces:
            parts = []
            for k in range(piece.shape[1] // 128):
                part = jnp.exp2((piece[:, k * 128:(k + 1) * 128] - mixed_top) * scale2)
                total = part if total is None else total + part
                parts.append(part.astype(jnp.bfloat16))
            weights.append(jnp.concatenate(parts, axis=1))
        totals = [
            jnp.sum(jnp.where(lax.rem(lane, heads) == h, total, 0.0), axis=1, keepdims=True)
            for h in range(heads)
        ]
        return tops, totals, weights

    with scope("leaf"):
        leaf_rows = leaf_slots * heads
        stats = []
        for b in range(owned):
            at = pl.ds(shared + b * leaf_rows, leaf_rows)
            scores = nt_dot(q_own[b * size:(b + 1) * size, :], keys[at, :])
            column = lax.broadcasted_iota(jnp.int32, scores.shape, 1)
            scores = jnp.where(column < leaf_len[b] * heads, scores, masked_score)
            tops, totals, weights = softmax_parts([scores], size)
            leaf_part[b * size:(b + 1) * size, :] = nn_dot(weights[0], values[at, :])
            stats.append(tops + totals)
        leaf_stats = to_lanes([
            jnp.concatenate([stats[b][k] for b in range(owned)], axis=0) for k in range(2 * heads)
        ])[0:8]

    group = max(1, min(n, ROWS // own_rows))
    rows = group * own_rows
    group_branches = group * owned
    groups = n // group

    def attend(i, carry):
        g = lax.rem(me // group + i, groups)

        def each(fn):
            for k in range(group):
                j = g * group + k
                pl.when(j != me)(functools.partial(fn, j))

        each(lambda j: remote(q_own, qall.at[j], q_s.at[j], q_r.at[j], "node", j).wait_recv())
        lows, highs = [], []
        for b in range(group_branches):
            mid = mid_of[g * group_branches + b]
            local = mid - me * local_mids
            here = (local >= 0) & (local < local_mids)
            low = local * (mid_slots * heads)
            highs.append(jnp.full((size, 128), jnp.where(here, low + mid_len[mid] * heads, 0), jnp.int32))
            lows.append(jnp.full((size, 128), jnp.where(here, low, 0), jnp.int32))
        low, high = jnp.concatenate(lows, axis=0), jnp.concatenate(highs, axis=0)
        query = qall[pl.ds(g * group, group)].reshape(rows, span)
        root_scores = nt_dot(query, keys[0:root, :])
        mid_scores = nt_dot(query, keys[root:shared, :])
        lane = lax.broadcasted_iota(jnp.int32, (rows, 128), 1)
        seen_scores = []
        for k in range(mids // 128):
            column = lane + k * 128
            seen = column < high
            if local_mids > 1:
                seen = seen & (column >= low)
            seen_scores.append(jnp.where(seen, mid_scores[:, k * 128:(k + 1) * 128], masked_score))
        tops, totals, weights = softmax_parts([root_scores] + seen_scores, rows)
        weighted = nn_dot(weights[0], values[0:root, :]) + nn_dot(
            jnp.concatenate(weights[1:], axis=1), values[root:shared, :]
        )
        part_send[pl.ds(g * group, group)] = weighted.astype(jnp.bfloat16).reshape(group, own_rows, span)
        st_send[g] = to_lanes(tops + totals)[0:8]

        def send(j):
            remote(part_send.at[j], part_recv.at[me], p_s.at[j], p_r.at[me], "node", j).start()
            remote(st_send.at[g], st_recv.at[me], t_s.at[j], t_r.at[me], "node", j).start()

        each(send)
        return carry

    with scope("attend"):
        lax.fori_loop(0, groups, attend, 0)
    part_recv[me] = part_send[me]
    st_recv[me] = st_send[me // group]
    with scope("partx"):
        wait_recvs("node", lambda j: part_send.at[j], part_recv, p_s, p_r)
        wait_recvs("node", lambda j: st_send.at[0], st_recv, t_s, t_r)

    with scope("merge"):
        blocks = []
        leaf_factors = []
        for h in range(heads):
            peak = jnp.concatenate([st_recv[i, h:h + 1, :] for i in range(n)], axis=0)
            total = jnp.concatenate([st_recv[i, heads + h:heads + h + 1, :] for i in range(n)], axis=0)
            leaf_peak, leaf_total = leaf_stats[h:h + 1], leaf_stats[heads + h:heads + h + 1]
            top = jnp.maximum(jnp.max(peak, axis=0, keepdims=True), leaf_peak)
            scale, leaf_scale = jnp.exp2((peak - top) * scale2), jnp.exp2((leaf_peak - top) * scale2)
            whole = jnp.sum(total * scale, axis=0, keepdims=True) + leaf_total * leaf_scale
            blocks.append(scale / whole)
            leaf_factors.append(leaf_scale / whole)
        used = heads * n + heads
        table = jnp.concatenate(
            blocks + leaf_factors + [jnp.zeros((128 - used, 128), jnp.float32)], axis=0
        )
        fac[...] = table.T
        mine = fac[pl.ds(pl.multiple_of(lax.rem(me, group) * own_rows, own_rows), own_rows), :]
        for h in range(heads):
            at = slice(h * hd, (h + 1) * hd)
            sum_h = leaf_part[:, at] * mine[:, heads * n + h:heads * n + h + 1]
            for i in range(n):
                sum_h = sum_h + part_recv[i, :, at].astype(jnp.float32) * mine[:, h * n + i:h * n + i + 1]
            att_own[:, at] = sum_h.astype(jnp.bfloat16)

    with scope("attag"):
        send_all("node", lambda j: att_own, att_all, a_s, a_r)
        att_all[me] = att_own[...]
        in_copies[1].wait()
        wait_recvs("node", lambda j: att_own, att_all, a_s, a_r)

    with scope("order"):
        mixed = nn_dot(order_ref[...], att_all[...].reshape(n * own_rows, span)).astype(jnp.bfloat16)
        for h in range(heads):
            for g in range(size):
                first = (h * size + g) * hd
                lhs[:, first:first + hd] = mixed[g * branches:(g + 1) * branches, h * hd:(h + 1) * hd]

    w_copies[0].wait()
    tiles, tile = pr_own.shape[0], pr_own.shape[2]

    def mp_peer(k):
        return lax.rem(mp_hi + k, mp_halves) * 2 + mp_lo

    def project(t, carry):
        at = pl.ds(pl.multiple_of(t * tile, tile), tile)
        value = nn_dot(lhs[...], ow[:, at])
        stream[:, at] = value
        pr_own[t] = value.astype(jnp.bfloat16)
        for k in range(1, mp_halves):
            peer = mp_peer(k)
            remote(
                pr_own.at[t], pr_hi.at[mp_hi, t], h_s.at[peer // 2, t], h_r.at[mp_hi, t], "mp", peer
            ).start()
        return carry

    def pair(t, carry):
        at = pl.ds(pl.multiple_of(t * tile, tile), tile)
        value = stream[:, at]
        for k in range(1, mp_halves):
            peer = mp_peer(k)
            at_hi = peer // 2
            remote(
                pr_own.at[t], pr_hi.at[at_hi, t], h_s.at[at_hi, t], h_r.at[at_hi, t], "mp", peer
            ).wait()
            value = value + pr_hi[at_hi, t].astype(jnp.float32)
        stream[:, at] = value
        pr_pair[t] = value.astype(jnp.bfloat16)
        remote(pr_pair.at[t], pr_lo.at[t], l_s.at[t], l_r.at[t], "mp", mp_partner).start()
        return carry

    def finish(t, squares):
        at = pl.ds(pl.multiple_of(t * tile, tile), tile)
        remote(pr_pair.at[t], pr_lo.at[t], l_s.at[t], l_r.at[t], "mp", mp_partner).wait()
        value = stream[:, at] + pr_lo[t].astype(jnp.float32) + res_ref[:, at].astype(jnp.float32)
        stream[:, at] = value
        xg[:, at] = (value * gain_ref[:, at]).astype(jnp.bfloat16)
        return squares + jnp.sum(value * value, axis=1, keepdims=True)

    with scope("project"):
        lax.fori_loop(0, tiles, project, 0)
    with scope("prhi"):
        in_copies[2].wait()
        in_copies[3].wait()
        lax.fori_loop(0, tiles, pair, 0)
    with scope("prlo"):
        squares = lax.fori_loop(0, tiles, finish, jnp.zeros((branches, 1), jnp.float32))
        sq_own[...] = to_lanes([squares])[0:8]
        send_all("node", lambda j: sq_own, sq_all, s_s, s_r)
        sq_all[me] = sq_own[...]

    with scope("wwait12"):
        w_copies[1].wait()
        w_copies[2].wait()

    def turn(i):
        down = jnp.where(owner_halves - 1 - i > hi, owner_halves - 1 - i, owner_halves - 2 - i)
        up = jnp.where(i < hi, i, i + 1)
        other = jnp.where(2 * hi >= owner_halves, up, down)
        return jnp.where((i == owner_halves - 1) & (hi < owner_halves), hi, other)

    def gate_up(j, off, count):
        at = pl.ds(pl.multiple_of(j * chunk + off, 128), count)
        return nn_dot(xg[...], gw[:, at]), nn_dot(xg[...], uw[:, at])

    def gx(k, s):
        at = pl.ds(subs[s][0], subs[s][1])
        return remote(
            gx_send.at[k, :, :, at], gx_recv.at[k, :, :, at], gx_s.at[k, s], gx_r.at[k, s], "node", partner
        )

    def gz(k, slot, s, recv_at):
        at = pl.ds(subs[s][0], subs[s][1])
        return remote(
            gz_send.at[k, :, :, at], gz_recv.at[slot, :, :, at], gz_s.at[k, s], gz_r.at[recv_at, s],
            "node", k * 2 + lo,
        )

    def partner_side(i, carry):
        k = turn(i)
        for s, (off, count) in enumerate(subs):
            gate, upward = gate_up(k * 2 + 1 - lo, off, count)
            gx_send[k, 0, :, off:off + count] = gate.astype(jnp.bfloat16)
            gx_send[k, 1, :, off:off + count] = upward.astype(jnp.bfloat16)
            gx(k, s).start()
        return carry

    def own_side(i, carry):
        k = turn(i)
        for s, (off, count) in enumerate(subs):
            at = slice(off, off + count)
            gate, upward = gate_up(k * 2 + lo, off, count)
            gx(k, s).wait_recv()
            gate = gate + gx_recv[k, 0, :, at].astype(jnp.float32)
            upward = upward + gx_recv[k, 1, :, at].astype(jnp.float32)

            @pl.when(k == hi)
            def _():
                own_sum[0, :, at] = gate
                own_sum[1, :, at] = upward

            @pl.when(k != hi)
            def _():
                gz_send[k, 0, :, at] = gate.astype(jnp.bfloat16)
                gz_send[k, 1, :, at] = upward.astype(jnp.bfloat16)
                gz(k, hi, s, hi).start()

        return carry

    with scope("gupartner"):
        lax.fori_loop(0, owner_halves, partner_side, 0)
    with scope("guown"):
        lax.fori_loop(0, owner_halves, own_side, 0)
    with scope("sqwait"):
        wait_recvs("node", lambda j: sq_own, sq_all, s_s, s_r)

    def act_z(k, owner, sem_at):
        return remote(
            act_all.at[owner], act_all.at[owner], cz_s.at[k], cz_r.at[sem_at], "node", k * 2 + lo
        )

    def act_x(k, side):
        owner = k * 2 + side
        return remote(act_all.at[owner], act_all.at[owner], cx_s.at[k], cx_r.at[k], "node", partner)

    def other_halves(fn):
        def body(i, carry):
            far = jnp.where(2 * hi >= halves, jnp.where(i < hi, i, i + 1),
                            jnp.where(halves - 1 - i > hi, halves - 1 - i, halves - 2 - i))
            fn(far)
            return carry

        lax.fori_loop(0, halves - 1, body, 0)

    def owner_work():
        total = sq_all[0]
        for k in range(1, n):
            total = total + sq_all[k]
        column = jnp.concatenate([total] * 16, axis=0).T[0:branches, 0:1]
        root_mean = lax.rsqrt(column / (width * n) + norm_eps)
        for s, (off, count) in enumerate(subs):
            at = slice(off, off + count)
            other_halves(lambda k: gz(0, k, s, k).wait_recv())

            def add(i, carry):
                k = lax.rem(hi + i, halves)
                return (
                    carry[0] + gz_recv[k, 0, :, at].astype(jnp.float32),
                    carry[1] + gz_recv[k, 1, :, at].astype(jnp.float32),
                )

            gate, upward = lax.fori_loop(1, halves, add, (own_sum[0, :, at], own_sum[1, :, at]))
            gate, upward = gate * root_mean, upward * root_mean
            act_all[me, :, at] = (gate / (1.0 + jnp.exp(-gate)) * upward).astype(jnp.bfloat16)
        act_x(hi, lo).start()
        other_halves(lambda k: act_z(k, me, hi).start())

    with scope("ownerwork"):
        if owners == n:
            owner_work()
        else:
            pl.when(me < owners)(owner_work)

    w_copies[3].wait()
    acc[...] = jnp.zeros(acc.shape, jnp.float32)

    def down(owner):
        at = pl.ds(pl.multiple_of(owner * chunk, 128), chunk)
        acc[...] += nn_dot(act_all[owner], dw[at, :])

    def down_own(i, carry):
        k = turn(owner_halves - 1 - i)

        @pl.when(k != hi)
        def _():
            act_z(k, k * 2 + lo, k).wait_recv()
            act_x(k, lo).start()

        down(k * 2 + lo)
        return carry

    def down_partner(i, carry):
        k = turn(owner_halves - 1 - i)
        act_x(k, 1 - lo).wait_recv()
        down(k * 2 + 1 - lo)
        return carry

    with scope("down1"):
        lax.fori_loop(0, owner_halves, down_own, 0)
    with scope("down2"):
        lax.fori_loop(0, owner_halves, down_partner, 0)

    rows_out = out_ref.shape[0]
    with scope("dnx"):
        for k in range(mp):
            dn_send[k] = acc[k * rows_out:(k + 1) * rows_out, :].astype(jnp.bfloat16)
        send_all("mp", lambda j: dn_send.at[j], dn_recv, d_s, d_r)
        dn_recv[mpi] = dn_send[mpi]
        wait_recvs("mp", lambda j: dn_send.at[j], dn_recv, d_s, d_r)
        total = dn_recv[0].astype(jnp.float32)
        for k in range(1, mp):
            total = total + dn_recv[k].astype(jnp.float32)
        own = stream[pl.ds(pl.multiple_of(mpi * rows_out, rows_out), rows_out), :]
        out_ref[...] = (own + total).astype(jnp.bfloat16)

    with scope("drain"):
        wait_sends("node", lambda j: q_own, qall, q_s, q_r)
        wait_sends("node", lambda j: part_send.at[j], part_recv, p_s, p_r)
        wait_sends("node", lambda j: st_send.at[0], st_recv, t_s, t_r)
        wait_sends("node", lambda j: att_own, att_all, a_s, a_r)
        wait_sends("node", lambda j: sq_own, sq_all, s_s, s_r)
        wait_sends("mp", lambda j: dn_send.at[j], dn_recv, d_s, d_r)

        def sent(k, carry):
            for s in range(len(subs)):
                gx(k, s).wait_send()
                pl.when(k != hi)(lambda s=s: gz(k, hi, s, hi).wait_send())
            act_x(k, lo).wait_send()
            return carry

        lax.fori_loop(0, owner_halves, sent, 0)

        def acts_sent():
            other_halves(lambda k: act_z(k, me, hi).wait_send())

        if owners == n:
            acts_sent()
        else:
            pl.when(me < owners)(acts_sent)


def on_device(
    n, mp,
    queries, root_keys, root_values, mid_keys, mid_values, leaf_keys, leaf_values,
    mid_length, leaf_length, branch_mid, residual, norm_gain,
    out_weight, gate_weight, up_weight, down_weight,
):
    owned, local_heads, hd = queries.shape
    heads = root_keys.shape[1]
    size = local_heads // heads
    own_rows = owned * size
    branches = owned * n
    width = residual.shape[1]
    hidden = gate_weight.shape[1]
    lane_tiles = hidden // 128
    owners = max(k for k in range(2, n + 1, 2) if lane_tiles % k == 0)
    chunk = hidden // owners
    first = (chunk // 128 + 1) // 2 * 128
    subs = ((0, first), (first, chunk - first)) if first < chunk else ((0, chunk),)
    mid_slots = mid_keys.shape[1]
    leaf_slots = leaf_keys.shape[1]
    local_mids = mid_keys.shape[0]
    halves, owner_halves, mp_halves = n // 2, owners // 2, mp // 2
    group = max(1, min(n, ROWS // own_rows))
    tile = math.gcd(width, 256)
    tiles = width // tile

    order = np.zeros((branches * size, branches * size), np.float32)
    at = np.arange(branches * size)
    order[(at % size) * branches + at // size, at] = 1.0

    flat = [
        a.reshape(-1, hd)
        for a in (root_keys, root_values, mid_keys, mid_values, leaf_keys, leaf_values)
    ]
    kv_rows = flat[0].shape[0] + flat[2].shape[0] + flat[4].shape[0]
    span = heads * hd
    bf, f32 = jnp.bfloat16, jnp.float32
    dma = pltpu.SemaphoreType.DMA
    vmem = pl.BlockSpec(memory_space=pltpu.VMEM)
    smem = pl.BlockSpec(memory_space=pltpu.SMEM)
    hbm = pl.BlockSpec(memory_space=pl.ANY)
    rows_out = branches // mp
    scratch = [
        pltpu.VMEM((owned, local_heads, hd), bf),
        pltpu.VMEM(order.shape, bf),
        pltpu.VMEM((branches, width), bf),
        pltpu.VMEM((1, width), f32),
        pltpu.VMEM((kv_rows, span), bf),
        pltpu.VMEM((kv_rows, span), bf),
        pltpu.VMEM(out_weight.shape, bf),
        pltpu.VMEM(gate_weight.shape, bf),
        pltpu.VMEM(up_weight.shape, bf),
        pltpu.VMEM(down_weight.shape, bf),
        pltpu.VMEM((own_rows, span), bf),
        pltpu.VMEM((n, own_rows, span), bf),
        pltpu.VMEM((n, own_rows, span), bf),
        pltpu.VMEM((n, own_rows, span), bf),
        pltpu.VMEM((n // group, 8, 128), f32),
        pltpu.VMEM((n, 8, 128), f32),
        pltpu.VMEM((own_rows, span), f32),
        pltpu.VMEM((128, 128), f32),
        pltpu.VMEM((own_rows, span), bf),
        pltpu.VMEM((n, own_rows, span), bf),
        pltpu.VMEM((branches, local_heads * hd), bf),
        pltpu.VMEM((tiles, branches, tile), bf),
        pltpu.VMEM((mp_halves, tiles, branches, tile), bf),
        pltpu.VMEM((tiles, branches, tile), bf),
        pltpu.VMEM((tiles, branches, tile), bf),
        pltpu.VMEM((branches, width), f32),
        pltpu.VMEM((8, 128), f32),
        pltpu.VMEM((n, 8, 128), f32),
        pltpu.VMEM((branches, width), bf),
        pltpu.VMEM((owner_halves, 2, branches, chunk), bf),
        pltpu.VMEM((owner_halves, 2, branches, chunk), bf),
        pltpu.VMEM((2, branches, chunk), f32),
        pltpu.VMEM((owner_halves, 2, branches, chunk), bf),
        pltpu.VMEM((halves, 2, branches, chunk), bf),
        pltpu.VMEM((owners, branches, chunk), bf),
        pltpu.VMEM((branches, width), f32),
        pltpu.VMEM((mp, rows_out, width), bf),
        pltpu.VMEM((mp, rows_out, width), bf),
        dma((4,)),
        dma((6,)),
        dma((4,)),
    ] + [dma((n,))] * 10 + [
        dma((mp_halves, tiles)),
        dma((mp_halves, tiles)),
        dma((tiles,)),
        dma((tiles,)),
        dma((owner_halves, len(subs))),
        dma((owner_halves, len(subs))),
        dma((owner_halves, len(subs))),
        dma((halves, len(subs))),
        dma((halves,)),
        dma((owner_halves,)),
        dma((owner_halves,)),
        dma((owner_halves,)),
        dma((mp,)),
        dma((mp,)),
    ]
    scale2 = hd ** -0.5 * math.log2(math.e)
    return pl.pallas_call(
        functools.partial(
            layer_kernel, n, mp, owners, scale2, local_mids, mid_slots, leaf_slots, size, subs
        ),
        out_shape=jax.ShapeDtypeStruct((rows_out, width), bf),
        in_specs=[smem] * 3 + [hbm] * 14,
        out_specs=vmem,
        scratch_shapes=scratch,
        compiler_params=pltpu.CompilerParams(
            collective_id=0, has_side_effects=True, vmem_limit_bytes=67043328
        ),
    )(
        branch_mid.reshape(-1), mid_length, leaf_length,
        queries, jnp.asarray(order, bf), residual, norm_gain[None, :],
        *flat, out_weight, gate_weight, up_weight, down_weight,
    )


def solution(mesh):
    in_specs = (
        P("node", "mp", None),
        P("node", "mp", None),
        P("node", "mp", None),
        P("node", None, "mp", None),
        P("node", None, "mp", None),
        P("node", None, "mp", None),
        P("node", None, "mp", None),
        P(),
        P("node"),
        P(),
        P(None, "node"),
        P("node"),
        P("mp", "node"),
        P("node", "mp"),
        P("node", "mp"),
        P("mp", "node"),
    )
    body = functools.partial(on_device, mesh.shape["node"], mesh.shape["mp"])
    return jax.shard_map(
        body, mesh=mesh, in_specs=in_specs, out_specs=P("mp", "node"), check_vma=False
    )
```

time: 105 us -> 64.4 us (0.61)
  the two profiles are of different devices: /device:TPU:19 before, /device:TPU:0 now
where the time goes in v1:
time: 64.4 us; the launch traced here: 64.1 us
  Pallas kernels  62.8 us (98%)
  local copies, waits for them, and re-layouts  1.32 us (2%)
    pallas_call x1, Pallas kernels, on_device(): pl.pallas_call(functools.partial(layer_kernel, n, mp, owners, scale2, loc...  62.8 us
    unnamed x1, local copies, waits for them, and re-layouts  1.32 us

profile of v1, /device:TPU:0, one launch (start us, length us, event | category | flops | bytes accessed | tf_op | source)
XLA Modules:
  0.0 64.1 jit_solution(17968514546494050081)
XLA Ops:
  0.0 62.8 %shard_map.163 = bf16[8,1024]{1,0:T(8,128)(2,1)} custom-call(s32[32]{0:T(128)} %bitcast.15, s32[8]{0:T(128)} %mid_len.1, s32[4]{0:T(128)} %leaf_len.1, bf16[4,16,128]{2,1,0:T(8,128)(2,1)} %q_hbm.1, bf16[256,256]{1,0:T(8,128)(2,1)} %constant.2.clone.order_hbm, bf16[32,1024]{1,0:T(8,128)(2,1)} %res_hbm.1, f32[1,1024]{1,0:T(1,128)} %bitcast.14, ...), custom_call_target="tpu_custom_call" | custom-call | tf_op jit(solution)/shard_map/pallas_call | solution.py:643
  62.8 1.3 %copy.19 = bf16[8,1024]{1,0:T(8,128)(2,1)} copy(bf16[8,1024]{1,0:T(8,128)(2,1)} %shard_map.163) | data formatting | bytes 32768

commit v2 on v1

v2 whole, which is shorter than its diff:
```python
import functools
import math
from contextlib import nullcontext as scope

import jax
import jax.numpy as jnp
import numpy as np
from jax import lax
from jax.experimental import pallas as pl
from jax.experimental.pallas import tpu as pltpu
from jax.sharding import PartitionSpec as P

norm_eps = 1e-05
masked_score = -1e30
MESH = pl.DeviceIdType.MESH
ROWS = 256


def nt_dot(a, b):
    return lax.dot_general(a, b, (((1,), (1,)), ((), ())), preferred_element_type=jnp.float32)


def nn_dot(a, b):
    return jnp.dot(a, b, preferred_element_type=jnp.float32)


def to_lanes(columns):
    rows = columns[0].shape[0]
    lane = lax.broadcasted_iota(jnp.int32, (rows, 128), 1)
    grid = jnp.zeros((rows, 128), jnp.float32)
    for k, column in enumerate(columns):
        grid = jnp.where(lane == k, column, grid)
    if rows < 128:
        grid = jnp.concatenate([grid] * (128 // rows), axis=0)
    return grid.T


def layer_kernel(
    n, mp, owners, scale2, local_mids, mid_slots, leaf_slots, size, subs,
    mid_of, mid_len, leaf_len,
    q_hbm, order_hbm, res_hbm, gain_hbm,
    rk_hbm, rv_hbm, mk_hbm, mv_hbm, lk_hbm, lv_hbm, ow_hbm, gw_hbm, uw_hbm, dw_hbm,
    out_ref,
    q_raw, order_ref, res_ref, gain_ref, keys, values, ow, gw, uw, dw,
    q_own, qall, part_send, part_recv, st_send, st_recv, leaf_part, fac, att_own, att_all, lhs,
    pr_own, pr_hi, pr_pair, pr_lo, stream, sq_own, sq_all, sq_own_scale, xg,
    gx_send, gx_recv, own_sum, gz_send, gz_recv, act_all, acc, dn_send, dn_recv,
    in_sem, kv_sem, w_sem, q_s, q_r, p_s, p_r, t_s, t_r, a_s, a_r, s_s, s_r,
    h_s, h_r, l_s, l_r, gx_s, gx_r, gz_s, gz_r, cz_s, cz_r, cx_s, cx_r, d_s, d_r,
):
    me = lax.axis_index("node")
    mpi = lax.axis_index("mp")
    owned, local_heads, hd = q_raw.shape
    heads = local_heads // size
    own_rows = owned * size
    span = heads * hd
    chunk = act_all.shape[2]
    branches, width = stream.shape
    root = rk_hbm.shape[0]
    mids = mk_hbm.shape[0]
    shared = root + mids
    lo, hi = lax.rem(me, 2), me // 2
    partner = me + 1 - 2 * lo
    halves = n // 2
    owner_halves = owners // 2
    mp_lo, mp_hi = lax.rem(mpi, 2), mpi // 2
    mp_partner = mpi + 1 - 2 * mp_lo
    mp_halves = mp // 2

    barrier = pltpu.get_barrier_semaphore()

    def greet(axis, here, count):
        def body(i, carry):
            pl.semaphore_signal(
                barrier, inc=1, device_id={axis: lax.rem(here + i, count)}, device_id_type=MESH
            )
            return carry

        lax.fori_loop(1, count, body, 0)

    greet("node", me, n)
    greet("mp", mpi, mp)

    in_copies = [
        pltpu.make_async_copy(src, dst, in_sem.at[k])
        for k, (src, dst) in enumerate(
            ((q_hbm, q_raw), (order_hbm, order_ref), (res_hbm, res_ref), (gain_hbm, gain_ref))
        )
    ]
    in_copies[0].start()
    for side, (dst, parts) in enumerate(
        ((keys, (rk_hbm, mk_hbm, lk_hbm)), (values, (rv_hbm, mv_hbm, lv_hbm)))
    ):
        start = 0
        for src in parts:
            rows = src.shape[0]
            pltpu.make_async_copy(
                src, dst.at[pl.ds(start, rows), pl.ds(0, hd)], kv_sem.at[side]
            ).start()
            start += rows
    for copy in in_copies[1:]:
        copy.start()
    w_copies = [
        pltpu.make_async_copy(src, dst, w_sem.at[k])
        for k, (src, dst) in enumerate(((ow_hbm, ow), (gw_hbm, gw), (uw_hbm, uw), (dw_hbm, dw)))
    ]

    def remote(src, dst, send, recv, axis, peer):
        return pltpu.make_async_remote_copy(
            src_ref=src, dst_ref=dst, send_sem=send, recv_sem=recv,
            device_id={axis: peer}, device_id_type=MESH,
        )

    def peers(axis, fn):
        here, count = (me, n) if axis == "node" else (mpi, mp)

        def body(i, carry):
            fn(lax.rem(here + i, count))
            return carry

        lax.fori_loop(1, count, body, 0)

    def send_all(axis, src, dst, send, recv):
        here = me if axis == "node" else mpi
        peers(axis, lambda j: remote(src(j), dst.at[here], send, recv, axis, j).start())

    def settle(ref, sem):
        pltpu.make_async_copy(ref, ref, sem).wait()

    def others(ref, count):
        return ref.at[pl.ds(0, count - 1)]

    with scope("qprep"):
        in_copies[0].wait()
        raw_q = q_raw[...].astype(jnp.float32)
        for h in range(heads):
            q_own[:, h * hd:(h + 1) * hd] = (
                raw_q[:, h * size:(h + 1) * size, :].reshape(own_rows, hd).astype(jnp.bfloat16)
            )
        qall[me] = q_own[...]

    with scope("barrier"):
        pl.semaphore_wait(barrier, n - 1 + mp - 1)
    group = max(1, min(n, ROWS // own_rows))
    groups = n // group

    def send_query(j):
        remote(q_own, qall.at[me], q_s, q_r.at[me // group], "node", j).start()

    def send_near(k, carry):
        send_query(me // group * group + lax.rem(me + k, group))
        return carry

    def send_far(k, carry):
        send_query(lax.rem(me // group * group + k, n))
        return carry

    lax.fori_loop(1, group, send_near, 0)
    lax.fori_loop(group, n, send_far, 0)

    with scope("kvwait"):
        for side, ref in enumerate((keys, values)):
            arrived = ref.at[:, pl.ds(0, hd)]
            pltpu.make_async_copy(arrived, arrived, kv_sem.at[side]).wait()
    for copy in w_copies:
        copy.start()

    block = math.gcd(512, math.gcd(shared, leaf_slots * heads))
    row = lax.broadcasted_iota(jnp.int32, (block, hd), 0)
    keep = [(lax.rem(row, heads) == h).astype(jnp.float32).astype(jnp.bfloat16) for h in range(heads)]

    def spread(i, carry):
        at = pl.ds(pl.multiple_of(i * block, block), block)
        for ref in (keys, values):
            mixed = ref[at, 0:hd]
            for h in range(heads):
                ref[at, h * hd:(h + 1) * hd] = mixed * keep[h]
        return carry

    with scope("spread"):
        lax.fori_loop(0, shared // block, spread, 0)

    def attend_rows(query, spans, seen):
        rows = query.shape[0]
        lane = lax.broadcasted_iota(jnp.int32, (rows, 128), 1)
        mine = [lax.rem(lane, heads) == h for h in range(heads)]

        def mix(columns):
            mixed = jnp.broadcast_to(columns[0], lane.shape)
            for h in range(1, heads):
                mixed = jnp.where(mine[h], columns[h], mixed)
            return mixed

        peaks, total, weighted = None, None, None
        for start, count in spans:
            scores = nt_dot(query, keys[start:start + count, :])
            parts = [
                seen(start + k, scores[:, k:k + 128], lane) for k in range(0, count, 128)
            ]
            top = functools.reduce(jnp.maximum, parts)
            now = [
                jnp.max(jnp.where(mine[h], top, -jnp.inf), axis=1, keepdims=True) for h in range(heads)
            ]
            if peaks is not None:
                now = [jnp.maximum(a, b) for a, b in zip(peaks, now)]
                shrink = [jnp.exp2((a - b) * scale2) for a, b in zip(peaks, now)]
                total = total * mix(shrink)
                weighted = weighted * jnp.concatenate(
                    [jnp.broadcast_to(a, (rows, hd)) for a in shrink], axis=1
                )
            peaks = now
            mixed = mix(peaks)
            rounded = []
            for part in parts:
                part = jnp.exp2((part - mixed) * scale2)
                total = part if total is None else total + part
                rounded.append(part.astype(jnp.bfloat16))
            product = nn_dot(jnp.concatenate(rounded, axis=1), values[start:start + count, :])
            weighted = product if weighted is None else weighted + product
        totals = [
            jnp.sum(jnp.where(mine[h], total, 0.0), axis=1, keepdims=True) for h in range(heads)
        ]
        return peaks, totals, weighted

    pack = min(group, 128 // own_rows)
    blocks = group // pack
    rows = group * own_rows
    group_branches = group * owned
    piece = math.gcd(2048, math.gcd(root, mids))

    def attend(i, carry):
        g = lax.rem(me // group + i, groups)

        def each(fn):
            for k in range(group):
                j = g * group + k
                pl.when(j != me)(functools.partial(fn, j))

        pl.when(g == me // group)(lambda: settle(qall.at[pl.ds(0, group - 1)], q_r.at[g]))
        if groups > 1:
            pl.when(g != me // group)(lambda: settle(qall.at[pl.ds(0, group)], q_r.at[g]))
        lows, highs = [], []
        for b in range(group_branches):
            mid = mid_of[g * group_branches + b]
            local = mid - me * local_mids
            here = (local >= 0) & (local < local_mids)
            low = local * (mid_slots * heads)
            highs.append(jnp.full((size, 128), jnp.where(here, low + mid_len[mid] * heads, 0), jnp.int32))
            lows.append(jnp.full((size, 128), jnp.where(here, low, 0), jnp.int32))
        low, high = jnp.concatenate(lows, axis=0), jnp.concatenate(highs, axis=0)
        query = qall[pl.ds(g * group, group)].reshape(rows, span)

        def seen(start, part, lane):
            if start < root:
                return part
            column = lane + (start - root)
            kept = column < high
            if local_mids > 1:
                kept = kept & (column >= low)
            return jnp.where(kept, part, masked_score)

        tops, totals, weighted = attend_rows(
            query, [(start, piece) for start in range(0, shared, piece)], seen
        )
        part_send[pl.ds(g * group, group)] = weighted.astype(jnp.bfloat16).reshape(group, own_rows, span)
        columns = tops + totals
        for k in range(blocks):
            at = slice(k * pack * own_rows, (k + 1) * pack * own_rows)
            st_send[g * blocks + k] = to_lanes([column[at] for column in columns])[0:8]

        def send(j):
            remote(part_send.at[j], part_recv.at[me], p_s, p_r, "node", j).start()
            remote(st_send.at[j // pack], st_recv.at[me], t_s, t_r, "node", j).start()

        each(send)
        return carry

    with scope("attend"):
        lax.fori_loop(0, groups, attend, 0)
    part_recv[me] = part_send[me]
    st_recv[me] = st_send[me // pack]

    with scope("leaf"):
        lax.fori_loop(shared // block, keys.shape[0] // block, spread, 0)
        leaf_rows = leaf_slots * heads
        stats = []
        for b in range(owned):
            start = shared + b * leaf_rows
            tops, totals, weighted = attend_rows(
                q_own[b * size:(b + 1) * size, :],
                [(start, leaf_rows)],
                lambda at, part, lane: jnp.where(
                    lane + (at - start) < leaf_len[b] * heads, part, masked_score
                ),
            )
            leaf_part[b * size:(b + 1) * size, :] = weighted
            stats.append(tops + totals)
        leaf_stats = to_lanes([
            jnp.concatenate([stats[b][k] for b in range(owned)], axis=0) for k in range(2 * heads)
        ])[0:8]

    with scope("partx"):
        settle(others(part_recv, n), p_r)
        settle(others(st_recv, n), t_r)

    with scope("merge"):
        factors = []
        leaf_factors = []
        for h in range(heads):
            peak = jnp.concatenate([st_recv[i, h:h + 1, :] for i in range(n)], axis=0)
            total = jnp.concatenate([st_recv[i, heads + h:heads + h + 1, :] for i in range(n)], axis=0)
            leaf_peak, leaf_total = leaf_stats[h:h + 1], leaf_stats[heads + h:heads + h + 1]
            top = jnp.maximum(jnp.max(peak, axis=0, keepdims=True), leaf_peak)
            scale, leaf_scale = jnp.exp2((peak - top) * scale2), jnp.exp2((leaf_peak - top) * scale2)
            whole = jnp.sum(total * scale, axis=0, keepdims=True) + leaf_total * leaf_scale
            factors.append(scale / whole)
            leaf_factors.append(leaf_scale / whole)
        used = heads * n + heads
        table = jnp.concatenate(
            factors + leaf_factors + [jnp.zeros((128 - used, 128), jnp.float32)], axis=0
        )
        fac[...] = table.T
        mine = fac[pl.ds(pl.multiple_of(lax.rem(me, pack) * own_rows, own_rows), own_rows), :]
        for h in range(heads):
            at = slice(h * hd, (h + 1) * hd)
            sum_h = leaf_part[:, at] * mine[:, heads * n + h:heads * n + h + 1]
            for i in range(n):
                sum_h = sum_h + part_recv[i, :, at].astype(jnp.float32) * mine[:, h * n + i:h * n + i + 1]
            att_own[:, at] = sum_h.astype(jnp.bfloat16)

    with scope("attag"):
        send_all("node", lambda j: att_own, att_all, a_s, a_r)
        att_all[me] = att_own[...]
        in_copies[1].wait()
        settle(others(att_all, n), a_r)

    with scope("order"):
        mixed = nn_dot(order_ref[...], att_all[...].reshape(n * own_rows, span)).astype(jnp.bfloat16)
        for h in range(heads):
            for g in range(size):
                first = (h * size + g) * hd
                lhs[:, first:first + hd] = mixed[g * branches:(g + 1) * branches, h * hd:(h + 1) * hd]

    w_copies[0].wait()
    tiles, tile = pr_own.shape[0], pr_own.shape[2]

    def mp_peer(k):
        return lax.rem(mp_hi + k, mp_halves) * 2 + mp_lo

    def project(t, carry):
        at = pl.ds(pl.multiple_of(t * tile, tile), tile)
        value = nn_dot(lhs[...], ow[:, at])
        stream[:, at] = value
        pr_own[t] = value.astype(jnp.bfloat16)
        for k in range(1, mp_halves):
            peer = mp_peer(k)
            remote(
                pr_own.at[t], pr_hi.at[mp_hi, t], h_s, h_r.at[mp_hi, t], "mp", peer
            ).start()
        return carry

    def pair(t, carry):
        at = pl.ds(pl.multiple_of(t * tile, tile), tile)
        value = stream[:, at]
        for k in range(1, mp_halves):
            peer = mp_peer(k)
            at_hi = peer // 2
            remote(
                pr_own.at[t], pr_hi.at[at_hi, t], h_s, h_r.at[at_hi, t], "mp", peer
            ).wait_recv()
            value = value + pr_hi[at_hi, t].astype(jnp.float32)
        stream[:, at] = value
        pr_pair[t] = value.astype(jnp.bfloat16)
        remote(pr_pair.at[t], pr_lo.at[t], l_s, l_r.at[t], "mp", mp_partner).start()
        return carry

    def finish(t, squares):
        at = pl.ds(pl.multiple_of(t * tile, tile), tile)
        remote(pr_pair.at[t], pr_lo.at[t], l_s, l_r.at[t], "mp", mp_partner).wait_recv()
        value = stream[:, at] + pr_lo[t].astype(jnp.float32) + res_ref[:, at].astype(jnp.float32)
        stream[:, at] = value
        xg[:, at] = (value * gain_ref[:, at]).astype(jnp.bfloat16)
        return squares + jnp.sum(value * value, axis=1, keepdims=True)

    with scope("project"):
        lax.fori_loop(0, tiles, project, 0)
    with scope("prhi"):
        in_copies[2].wait()
        in_copies[3].wait()
        lax.fori_loop(0, tiles, pair, 0)
    with scope("prlo"):
        squares = lax.fori_loop(0, tiles, finish, jnp.zeros((branches, 1), jnp.float32))

    def early_sent():
        settle(others(qall, n), q_s)
        settle(others(part_recv, n), p_s)
        settle(others(st_recv, n), t_s)
        settle(others(att_all, n), a_s)

    with scope("wwait12"):
        w_copies[1].wait()
        w_copies[2].wait()

    def turn(i):
        down = jnp.where(owner_halves - 1 - i > hi, owner_halves - 1 - i, owner_halves - 2 - i)
        up = jnp.where(i < hi, i, i + 1)
        other = jnp.where(2 * hi >= owner_halves, up, down)
        return jnp.where((i == owner_halves - 1) & (hi < owner_halves), hi, other)

    def gate_up(j, off, count):
        at = pl.ds(pl.multiple_of(j * chunk + off, 128), count)
        return nn_dot(xg[...], gw[:, at]), nn_dot(xg[...], uw[:, at])

    def gx(k, s):
        at = pl.ds(subs[s][0], subs[s][1])
        return remote(
            gx_send.at[k, :, :, at], gx_recv.at[k, :, :, at], gx_s, gx_r.at[k, s], "node", partner
        )

    def gz(k, target, slot, s):
        at = pl.ds(subs[s][0], subs[s][1])
        return remote(
            gz_send.at[k, :, :, at], gz_recv.at[slot, :, :, at], gz_s, gz_r.at[slot, s],
            "node", target * 2 + lo,
        )

    line = halves == 4 and owner_halves == 4
    outer = (hi == 0) | (hi == 3)
    beside = hi + 1 - 2 * lax.rem(hi, 2)
    across_outer = jnp.where(hi < 2, 3, 0)
    across_inner = jnp.where(hi < 2, 2, 1)
    line_turn = (
        across_outer,
        jnp.where(outer, across_inner, beside),
        jnp.where(outer, beside, across_inner),
        hi,
    )

    def partner_side(s, k):
        off, count = subs[s]
        gate, upward = gate_up(k * 2 + 1 - lo, off, count)
        gx_send[k, 0, :, off:off + count] = gate.astype(jnp.bfloat16)
        gx_send[k, 1, :, off:off + count] = upward.astype(jnp.bfloat16)
        gx(k, s).start()

    def own_side(s, k):
        off, count = subs[s]
        at = slice(off, off + count)
        gate, upward = gate_up(k * 2 + lo, off, count)
        gx(k, s).wait_recv()
        gate = gate + gx_recv[k, 0, :, at].astype(jnp.float32)
        upward = upward + gx_recv[k, 1, :, at].astype(jnp.float32)
        return gate, upward

    def keep_own(s, gate, upward):
        at = slice(subs[s][0], subs[s][0] + subs[s][1])
        own_sum[0, :, at] = gate
        own_sum[1, :, at] = upward

    def pass_on(s, k, target, slot, gate, upward):
        at = slice(subs[s][0], subs[s][0] + subs[s][1])
        gz_send[k, 0, :, at] = gate.astype(jnp.bfloat16)
        gz_send[k, 1, :, at] = upward.astype(jnp.bfloat16)
        gz(k, target, slot, s).start()

    def own_line(s, p):
        at = slice(subs[s][0], subs[s][0] + subs[s][1])
        k = line_turn[p]
        gate, upward = own_side(s, k)
        if p == 3:
            keep_own(s, gate, upward)
        elif p == 1:
            pass_on(s, k, beside, jnp.where(outer, 1, 2), gate, upward)
        else:
            held = p // 2

            @pl.when(outer)
            def _():
                pass_on(s, k, beside, p, gate, upward)

            @pl.when(jnp.logical_not(outer))
            def _():
                gz(k, beside, held, s).wait_recv()
                pass_on(
                    s, k, k, 3,
                    gate + gz_recv[held, 0, :, at].astype(jnp.float32),
                    upward + gz_recv[held, 1, :, at].astype(jnp.float32),
                )

    def own_direct(s, k):
        gate, upward = own_side(s, k)
        pl.when(k == hi)(lambda: keep_own(s, gate, upward))
        pl.when(k != hi)(lambda: pass_on(s, k, k, hi, gate, upward))

    def partner_turns(i, carry):
        for s in range(len(subs)):
            partner_side(s, turn(i))
        return carry

    def own_turns(i, carry):
        for s in range(len(subs)):
            own_direct(s, turn(i))
        return carry

    def act_z(k, s, owner, sem_at):
        at = pl.ds(subs[s][0], subs[s][1])
        return remote(
            act_all.at[owner, :, at], act_all.at[owner, :, at], cz_s, cz_r.at[sem_at, s],
            "node", k * 2 + lo,
        )

    def act_x(k, s, side):
        owner = k * 2 + side
        at = pl.ds(subs[s][0], subs[s][1])
        return remote(
            act_all.at[owner, :, at], act_all.at[owner, :, at], cx_s, cx_r.at[k, s], "node", partner
        )

    def other_halves(fn):
        def body(i, carry):
            down = jnp.where(halves - 1 - i > hi, halves - 1 - i, halves - 2 - i)
            fn(jnp.where(2 * hi >= halves, jnp.where(i < hi, i, i + 1), down))
            return carry

        lax.fori_loop(0, halves - 1, lambda i, carry: body(halves - 2 - i, carry), 0)

    def norm_scale():
        settle(others(sq_all, n), s_r)
        total = sq_all[0]
        for k in range(1, n):
            total = total + sq_all[k]
        mean = total / (width * n)
        sq_own_scale[...] = jnp.concatenate([lax.rsqrt(mean + norm_eps)] * 16, axis=0).T

    def owner_work(s):
        off, count = subs[s]
        at = slice(off, off + count)
        root_mean = sq_own_scale[0:branches, 0:1]

        def add(k, carry):
            return (
                carry[0] + gz_recv[k, 0, :, at].astype(jnp.float32),
                carry[1] + gz_recv[k, 1, :, at].astype(jnp.float32),
            )

        gate, upward = own_sum[0, :, at], own_sum[1, :, at]
        if line:
            for slot in (2, 3):
                gz(0, beside, slot, s).wait_recv()
                gate, upward = add(slot, (gate, upward))
        else:
            other_halves(lambda k: gz(0, k, k, s).wait_recv())
            gate, upward = lax.fori_loop(
                1, halves, lambda i, carry: add(lax.rem(hi + i, halves), carry), (gate, upward)
            )
        gate, upward = gate * root_mean, upward * root_mean
        act_all[me, :, at] = (gate / (1.0 + jnp.exp(-gate)) * upward).astype(jnp.bfloat16)
        act_x(hi, s, lo).start()
        other_halves(lambda k: act_z(k, s, me, hi).start())

    def own_act(s):
        if owners == n:
            owner_work(s)
        else:
            pl.when(me < owners)(functools.partial(owner_work, s))

    def down(owner, s):
        off, count = subs[s]
        at = pl.ds(pl.multiple_of(owner * chunk + off, 128), count)
        acc[...] += nn_dot(act_all[owner, :, off:off + count], dw[at, :])

    def forward(i, carry):
        k = turn(owner_halves - 1 - i)
        for s in range(steps):
            @pl.when(k != hi)
            def _():
                act_z(k, s, k * 2 + lo, k).wait_recv()
                act_x(k, s, lo).start()

        for s in range(steps):
            down(k * 2 + lo, s)
        return carry

    def from_partner(i, carry):
        k = turn(owner_halves - 1 - i)
        for s in range(steps):
            act_x(k, s, 1 - lo).wait_recv()
            down(k * 2 + 1 - lo, s)
        return carry

    steps = len(subs)
    acc[...] = jnp.zeros(acc.shape, jnp.float32)
    with scope("gupartner"):
        if line:
            for p in range(4):
                for s in range(steps):
                    partner_side(s, line_turn[p])
        else:
            lax.fori_loop(0, owner_halves, partner_turns, 0)
    with scope("sqsend"):
        sq_own[...] = to_lanes([squares])[0:8]
        send_all("node", lambda j: sq_own, sq_all, s_s, s_r)
        sq_all[me] = sq_own[...]
        early_sent()
    if line:
        for p in range(4):
            for s in range(steps):
                with scope(f"own{p}{s}"):
                    own_line(s, p)
    else:
        lax.fori_loop(0, owner_halves, own_turns, 0)
    with scope("norm"):
        norm_scale()
    w_copies[3].wait()
    for s in range(steps):
        with scope(f"act{s}"):
            own_act(s)
    with scope("forward"):
        lax.fori_loop(0, owner_halves, forward, 0)
    with scope("frompartner"):
        lax.fori_loop(0, owner_halves, from_partner, 0)

    rows_out = out_ref.shape[0]
    with scope("dnx"):
        for k in range(mp):
            dn_send[k] = acc[k * rows_out:(k + 1) * rows_out, :].astype(jnp.bfloat16)
        send_all("mp", lambda j: dn_send.at[j], dn_recv, d_s, d_r)
        dn_recv[mpi] = dn_send[mpi]
        settle(others(sq_all, n), s_s)
        for _ in range(1, mp_halves):
            settle(pr_own, h_s)
        settle(pr_pair, l_s)
        settle(gx_send, gx_s)
        settle(act_all.at[pl.ds(0, owner_halves)], cx_s)
        if owners == n:
            settle(others(gz_send, owner_halves), gz_s)
            settle(act_all.at[pl.ds(0, halves - 1)], cz_s)
        else:
            owning = hi < owner_halves
            pl.when(owning)(lambda: settle(others(gz_send, owner_halves), gz_s))
            pl.when(owning)(lambda: settle(act_all.at[pl.ds(0, halves - 1)], cz_s))
            pl.when(jnp.logical_not(owning))(lambda: settle(gz_send, gz_s))
        settle(others(dn_recv, mp), d_r)
        total = dn_recv[0].astype(jnp.float32)
        for k in range(1, mp):
            total = total + dn_recv[k].astype(jnp.float32)
        own = stream[pl.ds(pl.multiple_of(mpi * rows_out, rows_out), rows_out), :]
        out_ref[...] = (own + total).astype(jnp.bfloat16)

    with scope("drain"):
        settle(others(dn_recv, mp), d_s)


def on_device(
    n, mp,
    queries, root_keys, root_values, mid_keys, mid_values, leaf_keys, leaf_values,
    mid_length, leaf_length, branch_mid, residual, norm_gain,
    out_weight, gate_weight, up_weight, down_weight,
):
    owned, local_heads, hd = queries.shape
    heads = root_keys.shape[1]
    size = local_heads // heads
    own_rows = owned * size
    branches = owned * n
    width = residual.shape[1]
    hidden = gate_weight.shape[1]
    lane_tiles = hidden // 128
    owners = max(k for k in range(2, n + 1, 2) if lane_tiles % k == 0)
    chunk = hidden // owners
    first = (chunk // 128 + 1) // 2 * 128
    subs = ((0, first), (first, chunk - first)) if first < chunk else ((0, chunk),)
    mid_slots = mid_keys.shape[1]
    leaf_slots = leaf_keys.shape[1]
    local_mids = mid_keys.shape[0]
    halves, owner_halves, mp_halves = n // 2, owners // 2, mp // 2
    group = max(1, min(n, ROWS // own_rows))
    pack = min(group, 128 // own_rows)
    tile = math.gcd(width, 256)
    tiles = width // tile

    order = np.zeros((branches * size, branches * size), np.float32)
    at = np.arange(branches * size)
    order[(at % size) * branches + at // size, at] = 1.0

    flat = [
        a.reshape(-1, hd)
        for a in (root_keys, root_values, mid_keys, mid_values, leaf_keys, leaf_values)
    ]
    kv_rows = flat[0].shape[0] + flat[2].shape[0] + flat[4].shape[0]
    span = heads * hd
    bf, f32 = jnp.bfloat16, jnp.float32
    dma = pltpu.SemaphoreType.DMA
    vmem = pl.BlockSpec(memory_space=pltpu.VMEM)
    smem = pl.BlockSpec(memory_space=pltpu.SMEM)
    hbm = pl.BlockSpec(memory_space=pl.ANY)
    rows_out = branches // mp
    scratch = [
        pltpu.VMEM((owned, local_heads, hd), bf),
        pltpu.VMEM(order.shape, bf),
        pltpu.VMEM((branches, width), bf),
        pltpu.VMEM((1, width), f32),
        pltpu.VMEM((kv_rows, span), bf),
        pltpu.VMEM((kv_rows, span), bf),
        pltpu.VMEM(out_weight.shape, bf),
        pltpu.VMEM(gate_weight.shape, bf),
        pltpu.VMEM(up_weight.shape, bf),
        pltpu.VMEM(down_weight.shape, bf),
        pltpu.VMEM((own_rows, span), bf),
        pltpu.VMEM((n, own_rows, span), bf),
        pltpu.VMEM((n, own_rows, span), bf),
        pltpu.VMEM((n, own_rows, span), bf),
        pltpu.VMEM((n // pack, 8, 128), f32),
        pltpu.VMEM((n, 8, 128), f32),
        pltpu.VMEM((own_rows, span), f32),
        pltpu.VMEM((128, 128), f32),
        pltpu.VMEM((own_rows, span), bf),
        pltpu.VMEM((n, own_rows, span), bf),
        pltpu.VMEM((branches, local_heads * hd), bf),
        pltpu.VMEM((tiles, branches, tile), bf),
        pltpu.VMEM((mp_halves, tiles, branches, tile), bf),
        pltpu.VMEM((tiles, branches, tile), bf),
        pltpu.VMEM((tiles, branches, tile), bf),
        pltpu.VMEM((branches, width), f32),
        pltpu.VMEM((8, 128), f32),
        pltpu.VMEM((n, 8, 128), f32),
        pltpu.VMEM((128, 128), f32),
        pltpu.VMEM((branches, width), bf),
        pltpu.VMEM((owner_halves, 2, branches, chunk), bf),
        pltpu.VMEM((owner_halves, 2, branches, chunk), bf),
        pltpu.VMEM((2, branches, chunk), f32),
        pltpu.VMEM((owner_halves, 2, branches, chunk), bf),
        pltpu.VMEM((halves, 2, branches, chunk), bf),
        pltpu.VMEM((owners, branches, chunk), bf),
        pltpu.VMEM((branches, width), f32),
        pltpu.VMEM((mp, rows_out, width), bf),
        pltpu.VMEM((mp, rows_out, width), bf),
        dma((4,)),
        dma((2,)),
        dma((4,)),
        dma(()),
        dma((n // group,)),
    ] + [dma(())] * 8 + [
        dma(()),
        dma((mp_halves, tiles)),
        dma(()),
        dma((tiles,)),
        dma(()),
        dma((owner_halves, len(subs))),
        dma(()),
        dma((halves, len(subs))),
        dma(()),
        dma((owner_halves, len(subs))),
        dma(()),
        dma((owner_halves, len(subs))),
        dma(()),
        dma(()),
    ]
    scale2 = hd ** -0.5 * math.log2(math.e)
    return pl.pallas_call(
        functools.partial(
            layer_kernel, n, mp, owners, scale2, local_mids, mid_slots, leaf_slots, size, subs
        ),
        out_shape=pltpu.VMEM((rows_out, width), bf),
        in_specs=[smem] * 3 + [hbm] * 14,
        out_specs=vmem,
        scratch_shapes=scratch,
        compiler_params=pltpu.CompilerParams(
            collective_id=0, has_side_effects=True, vmem_limit_bytes=66900000
        ),
    )(
        branch_mid.reshape(-1), mid_length, leaf_length,
        queries, jnp.asarray(order, bf), residual, norm_gain[None, :],
        *flat, out_weight, gate_weight, up_weight, down_weight,
    )


def solution(mesh):
    in_specs = (
        P("node", "mp", None),
        P("node", "mp", None),
        P("node", "mp", None),
        P("node", None, "mp", None),
        P("node", None, "mp", None),
        P("node", None, "mp", None),
        P("node", None, "mp", None),
        P(),
        P("node"),
        P(),
        P(None, "node"),
        P("node"),
        P("mp", "node"),
        P("node", "mp"),
        P("node", "mp"),
        P("mp", "node"),
    )
    body = functools.partial(on_device, mesh.shape["node"], mesh.shape["mp"])
    return jax.shard_map(
        body, mesh=mesh, in_specs=in_specs, out_specs=P("mp", "node"), check_vma=False
    )
```

time: 64.4 us -> 57.8 us (0.90)
  Pallas kernels: 62.8 us -> 57 us
  local copies, waits for them, and re-layouts: 1.32 us -> 0.61 us
    pallas_call x1, Pallas kernels: 62.8 us -> 57 us  [on_device(): pl.pallas_call(functools.partial(layer_kernel, n, mp, owners, scale2, loc...]
    unnamed x1, local copies, waits for them, and re-layouts: 1.32 us -> 0.61 us
where the time goes in v2:
time: 57.8 us; the launch traced here: 57.6 us
  Pallas kernels  57 us (99%)
  local copies, waits for them, and re-layouts  0.61 us (1%)
    pallas_call x1, Pallas kernels, on_device(): pl.pallas_call(functools.partial(layer_kernel, n, mp, owners, scale2, loc...  57 us

profile of v2, /device:TPU:0, one launch (start us, length us, event | category | flops | bytes accessed | tf_op | source)
XLA Modules:
  0.0 57.6 jit_solution(11129408243415330848)
XLA Ops:
  0.0 57.0 %shard_map.163 = bf16[8,1024]{1,0:T(8,128)(2,1)S(1)} custom-call(s32[32]{0:T(128)} %bitcast.15, s32[8]{0:T(128)} %mid_len.1, s32[4]{0:T(128)} %leaf_len.1, bf16[4,16,128]{2,1,0:T(8,128)(2,1)} %q_hbm.1, bf16[256,256]{1,0:T(8,128)(2,1)} %constant.2.clone.order_hbm, bf16[32,1024]{1,0:T(8,128)(2,1)} %res_hbm.1, f32[1,1024]{1,0:T(1,128)} %bitcast.14, ...), custom_call_target="tpu_custom_call" | custom-call | tf_op jit(solution)/shard_map/pallas_call | solution.py:759
  57.0 0.6 %copy.19 = bf16[8,1024]{1,0:T(8,128)(2,1)} copy(bf16[8,1024]{1,0:T(8,128)(2,1)S(1)} %shard_map.163) | data formatting | bytes 32768

commit v3 on v2

--- a/solution.py
+++ b/solution.py
@@ -14,6 +14,7 @@
 masked_score = -1e30
 MESH = pl.DeviceIdType.MESH
 ROWS = 256
+PIECES = 2
 
 
 def nt_dot(a, b):
@@ -37,11 +38,10 @@
 
 def layer_kernel(
     n, mp, owners, scale2, local_mids, mid_slots, leaf_slots, size, subs,
-    mid_of, mid_len, leaf_len,
-    q_hbm, order_hbm, res_hbm, gain_hbm,
+    mid_of_hbm, mid_len_hbm, leaf_len_hbm, q_hbm, order_hbm, res_hbm, gain_hbm,
     rk_hbm, rv_hbm, mk_hbm, mv_hbm, lk_hbm, lv_hbm, ow_hbm, gw_hbm, uw_hbm, dw_hbm,
     out_ref,
-    q_raw, order_ref, res_ref, gain_ref, keys, values, ow, gw, uw, dw,
+    mid_of, mid_len, leaf_len, q_raw, order_ref, res_ref, gain_ref, keys, values, ow, gw, uw, dw,
     q_own, qall, part_send, part_recv, st_send, st_recv, leaf_part, fac, att_own, att_all, lhs,
     pr_own, pr_hi, pr_pair, pr_lo, stream, sq_own, sq_all, sq_own_scale, xg,
     gx_send, gx_recv, own_sum, gz_send, gz_recv, act_all, acc, dn_send, dn_recv,
@@ -67,6 +67,16 @@
     mp_partner = mpi + 1 - 2 * mp_lo
     mp_halves = mp // 2
 
+    in_copies = [
+        pltpu.make_async_copy(src, dst, in_sem.at[k])
+        for k, (src, dst) in enumerate(
+            (
+                (q_hbm, q_raw), (order_hbm, order_ref), (res_hbm, res_ref), (gain_hbm, gain_ref),
+                (mid_of_hbm, mid_of), (mid_len_hbm, mid_len), (leaf_len_hbm, leaf_len),
+            )
+        )
+    ]
+    in_copies[0].start()
     barrier = pltpu.get_barrier_semaphore()
 
     def greet(axis, here, count):
@@ -80,14 +90,6 @@
 
     greet("node", me, n)
     greet("mp", mpi, mp)
-
-    in_copies = [
-        pltpu.make_async_copy(src, dst, in_sem.at[k])
-        for k, (src, dst) in enumerate(
-            ((q_hbm, q_raw), (order_hbm, order_ref), (res_hbm, res_ref), (gain_hbm, gain_ref))
-        )
-    ]
-    in_copies[0].start()
     for side, (dst, parts) in enumerate(
         ((keys, (rk_hbm, mk_hbm, lk_hbm)), (values, (rv_hbm, mv_hbm, lv_hbm)))
     ):
@@ -159,6 +161,8 @@
     lax.fori_loop(group, n, send_far, 0)
 
     with scope("kvwait"):
+        for copy in in_copies[4:]:
+            copy.wait()
         for side, ref in enumerate((keys, values)):
             arrived = ref.at[:, pl.ds(0, hd)]
             pltpu.make_async_copy(arrived, arrived, kv_sem.at[side]).wait()
@@ -233,7 +237,7 @@
 
         def each(fn):
             for k in range(group):
-                j = g * group + k
+                j = g * group + lax.rem(me - g * group + group // 2 + k + group, group)
                 pl.when(j != me)(functools.partial(fn, j))
 
         pl.when(g == me // group)(lambda: settle(qall.at[pl.ds(0, group - 1)], q_r.at[g]))
@@ -569,7 +573,7 @@
         at = pl.ds(pl.multiple_of(owner * chunk + off, 128), count)
         acc[...] += nn_dot(act_all[owner, :, off:off + count], dw[at, :])
 
-    def forward(i, carry):
+    def forward_turns(i, carry):
         k = turn(owner_halves - 1 - i)
         for s in range(steps):
             @pl.when(k != hi)
@@ -581,7 +585,7 @@
             down(k * 2 + lo, s)
         return carry
 
-    def from_partner(i, carry):
+    def partner_acts(i, carry):
         k = turn(owner_halves - 1 - i)
         for s in range(steps):
             act_x(k, s, 1 - lo).wait_recv()
@@ -604,21 +608,22 @@
         early_sent()
     if line:
         for p in range(4):
+            if p == 3:
+                norm_scale()
             for s in range(steps):
                 with scope(f"own{p}{s}"):
                     own_line(s, p)
     else:
         lax.fori_loop(0, owner_halves, own_turns, 0)
-    with scope("norm"):
         norm_scale()
     w_copies[3].wait()
     for s in range(steps):
         with scope(f"act{s}"):
             own_act(s)
     with scope("forward"):
-        lax.fori_loop(0, owner_halves, forward, 0)
+        lax.fori_loop(0, owner_halves, forward_turns, 0)
     with scope("frompartner"):
-        lax.fori_loop(0, owner_halves, from_partner, 0)
+        lax.fori_loop(0, owner_halves, partner_acts, 0)
 
     rows_out = out_ref.shape[0]
     with scope("dnx"):
@@ -667,8 +672,12 @@
     lane_tiles = hidden // 128
     owners = max(k for k in range(2, n + 1, 2) if lane_tiles % k == 0)
     chunk = hidden // owners
-    first = (chunk // 128 + 1) // 2 * 128
-    subs = ((0, first), (first, chunk - first)) if first < chunk else ((0, chunk),)
+    subs, off = [], 0
+    for left in range(PIECES, 0, -1):
+        count = -(-(chunk - off) // (128 * left)) * 128
+        if count:
+            subs.append((off, count))
+        off += count
     mid_slots = mid_keys.shape[1]
     leaf_slots = leaf_keys.shape[1]
     local_mids = mid_keys.shape[0]
@@ -691,10 +700,12 @@
     bf, f32 = jnp.bfloat16, jnp.float32
     dma = pltpu.SemaphoreType.DMA
     vmem = pl.BlockSpec(memory_space=pltpu.VMEM)
-    smem = pl.BlockSpec(memory_space=pltpu.SMEM)
     hbm = pl.BlockSpec(memory_space=pl.ANY)
     rows_out = branches // mp
     scratch = [
+        pltpu.SMEM(branch_mid.shape[:1], jnp.int32),
+        pltpu.SMEM(mid_length.shape, jnp.int32),
+        pltpu.SMEM(leaf_length.shape, jnp.int32),
         pltpu.VMEM((owned, local_heads, hd), bf),
         pltpu.VMEM(order.shape, bf),
         pltpu.VMEM((branches, width), bf),
@@ -734,7 +745,7 @@
         pltpu.VMEM((branches, width), f32),
         pltpu.VMEM((mp, rows_out, width), bf),
         pltpu.VMEM((mp, rows_out, width), bf),
-        dma((4,)),
+        dma((7,)),
         dma((2,)),
         dma((4,)),
         dma(()),
@@ -761,7 +772,7 @@
             layer_kernel, n, mp, owners, scale2, local_mids, mid_slots, leaf_slots, size, subs
         ),
         out_shape=pltpu.VMEM((rows_out, width), bf),
-        in_specs=[smem] * 3 + [hbm] * 14,
+        in_specs=[hbm] * 17,
         out_specs=vmem,
         scratch_shapes=scratch,
         compiler_params=pltpu.CompilerParams(

time: 57.8 us -> 57.4 us (level)
  no operation moved by 1% of the time
where the time goes in v3:
time: 57.4 us; the launch traced here: 57.2 us
  Pallas kernels  56.6 us (99%)
  local copies, waits for them, and re-layouts  0.61 us (1%)
    pallas_call x1, Pallas kernels, on_device(): pl.pallas_call(functools.partial(layer_kernel, n, mp, owners, scale2, loc...  56.6 us

profile of v3, /device:TPU:0, one launch (start us, length us, event | category | flops | bytes accessed | tf_op | source)
XLA Modules:
  0.0 57.2 jit_solution(3405548563444629543)
XLA Ops:
  0.0 56.6 %shard_map.163 = bf16[8,1024]{1,0:T(8,128)(2,1)S(1)} custom-call(s32[32]{0:T(128)} %bitcast.15, s32[8]{0:T(128)} %mid_len_hbm.1, s32[4]{0:T(128)} %leaf_len_hbm.1, bf16[4,16,128]{2,1,0:T(8,128)(2,1)} %q_hbm.1, bf16[256,256]{1,0:T(8,128)(2,1)} %constant.2.clone.order_hbm, bf16[32,1024]{1,0:T(8,128)(2,1)} %res_hbm.1, f32[1,1024]{1,0:T(1,128)} %bitcast.14, ...), custom_call_target="tpu_custom_call" | custom-call | tf_op jit(solution)/shard_map/pallas_call | solution.py:770
  56.6 0.6 %copy.19 = bf16[8,1024]{1,0:T(8,128)(2,1)} copy(bf16[8,1024]{1,0:T(8,128)(2,1)S(1)} %shard_map.163) | data formatting | bytes 32768

commit v4 on v3

--- a/solution.py
+++ b/solution.py
@@ -434,8 +434,8 @@
     across_outer = jnp.where(hi < 2, 3, 0)
     across_inner = jnp.where(hi < 2, 2, 1)
     line_turn = (
-        across_outer,
-        jnp.where(outer, across_inner, beside),
+        jnp.where(outer, across_outer, beside),
+        jnp.where(outer, across_inner, across_outer),
         jnp.where(outer, beside, across_inner),
         hi,
     )
@@ -473,10 +473,10 @@
         gate, upward = own_side(s, k)
         if p == 3:
             keep_own(s, gate, upward)
-        elif p == 1:
-            pass_on(s, k, beside, jnp.where(outer, 1, 2), gate, upward)
+        elif p == 0:
+            pass_on(s, k, beside, jnp.where(outer, 0, 2), gate, upward)
         else:
-            held = p // 2
+            held = p - 1
 
             @pl.when(outer)
             def _():

time: 57.4 us -> 57.4 us (level)
  no operation moved by 1% of the time
where the time goes in v4:
time: 57.4 us; the launch traced here: 57.1 us
  Pallas kernels  56.5 us (98%)
  local copies, waits for them, and re-layouts  0.61 us (1%)
    pallas_call x1, Pallas kernels, on_device(): pl.pallas_call(functools.partial(layer_kernel, n, mp, owners, scale2, loc...  56.5 us

profile of v4, /device:TPU:0, one launch (start us, length us, event | category | flops | bytes accessed | tf_op | source)
XLA Modules:
  0.0 57.1 jit_solution(10914292682260638798)
XLA Ops:
  0.0 56.5 %shard_map.163 = bf16[8,1024]{1,0:T(8,128)(2,1)S(1)} custom-call(s32[32]{0:T(128)} %bitcast.15, s32[8]{0:T(128)} %mid_len_hbm.1, s32[4]{0:T(128)} %leaf_len_hbm.1, bf16[4,16,128]{2,1,0:T(8,128)(2,1)} %q_hbm.1, bf16[256,256]{1,0:T(8,128)(2,1)} %constant.2.clone.order_hbm, bf16[32,1024]{1,0:T(8,128)(2,1)} %res_hbm.1, f32[1,1024]{1,0:T(1,128)} %bitcast.14, ...), custom_call_target="tpu_custom_call" | custom-call | tf_op jit(solution)/shard_map/pallas_call | solution.py:770
  56.5 0.6 %copy.19 = bf16[8,1024]{1,0:T(8,128)(2,1)} copy(bf16[8,1024]{1,0:T(8,128)(2,1)S(1)} %shard_map.163) | data formatting | bytes 32768

commit v5 on v4

--- a/solution.py
+++ b/solution.py
@@ -237,7 +237,7 @@
 
         def each(fn):
             for k in range(group):
-                j = g * group + lax.rem(me - g * group + group // 2 + k + group, group)
+                j = g * group + lax.rem(me + group // 2 + k, group)
                 pl.when(j != me)(functools.partial(fn, j))
 
         pl.when(g == me // group)(lambda: settle(qall.at[pl.ds(0, group - 1)], q_r.at[g]))

time: 57.4 us -> 57.4 us (level)
  no operation moved by 1% of the time
where the time goes in v5:
time: 57.4 us; the launch traced here: 57.1 us
  Pallas kernels  56.5 us (98%)
  local copies, waits for them, and re-layouts  0.61 us (1%)
    pallas_call x1, Pallas kernels, on_device(): pl.pallas_call(functools.partial(layer_kernel, n, mp, owners, scale2, loc...  56.5 us

profile of v5, /device:TPU:0, one launch (start us, length us, event | category | flops | bytes accessed | tf_op | source)
XLA Modules:
  0.0 57.1 jit_solution(12852572638312932063)
XLA Ops:
  0.0 56.5 %shard_map.163 = bf16[8,1024]{1,0:T(8,128)(2,1)S(1)} custom-call(s32[32]{0:T(128)} %bitcast.15, s32[8]{0:T(128)} %mid_len_hbm.1, s32[4]{0:T(128)} %leaf_len_hbm.1, bf16[4,16,128]{2,1,0:T(8,128)(2,1)} %q_hbm.1, bf16[256,256]{1,0:T(8,128)(2,1)} %constant.2.clone.order_hbm, bf16[32,1024]{1,0:T(8,128)(2,1)} %res_hbm.1, f32[1,1024]{1,0:T(1,128)} %bitcast.14, ...), custom_call_target="tpu_custom_call" | custom-call | tf_op jit(solution)/shard_map/pallas_call | solution.py:770
  56.5 0.6 %copy.19 = bf16[8,1024]{1,0:T(8,128)(2,1)} copy(bf16[8,1024]{1,0:T(8,128)(2,1)S(1)} %shard_map.163) | data formatting | bytes 32768
